TPU v7x, 512 devices: a whole 4x8x8 slice. The times are simulated.
512 devices in a mesh: req: 16 (over y, core), exp: 32 (over z, x).
Axes of the slice: x: 4, y: 8, z: 8, core: 2. Of those that a mesh axis runs over, the one named last changes fastest.
Arguments:
- new_q: bfloat16 [65536, 2048], P(('req', 'exp')), may hold values from -118 to 118
- new_kv: bfloat16 [65536, 4096], P(('req', 'exp')), may hold values from -4.5 to 4.5
- cache_kv: bfloat16 [65536, 4096], P(('req', 'exp')), may hold values from -4.6 to 4.6
- cache_len: int32 [512], P(('req', 'exp')), may hold values from 2 to 128
- prompt_kv: bfloat16 [4096, 4096], P(('req', 'exp')), may hold values from -4.5 to 4.5
- prompt_len: int32 [512], P(('req', 'exp')), may hold values from 1 to 8
- residual: bfloat16 [65536, 2048], P(('req', 'exp')), may hold values from -40 to 40
- norm_gain: float32 [2048], replicated, may hold values from 0.5 to 1.5
- routes: int32 [65536, 4], P(('req', 'exp')), may hold values from 0 to 31, all different within a row; in each aligned block of 128 rows (0 to 127, 128 to 255, ...) at most 20 rows name the same one
- route_weight: float32 [65536, 4], P(('req', 'exp')), may hold values from 0.1 to 1
- gate_up: bfloat16 [32, 2048, 1536], P('exp', 'req'), may hold values from -0.125 to 0.125
- down_proj: bfloat16 [32, 768, 2048], P('exp', None, 'req'), may hold values from -0.21875 to 0.21875
Outputs:
- layer_out: bfloat16 [65536, 2048], P(('req', 'exp'))
Inputs may be any that keep to these rules, and one draw needn't show every extreme that they name: `routes`: each row names 4 different experts; among the rows of one request no expert is named more than 20 times.
All inputs are finite; a program needn't handle non-finite values.
Results may differ from a plain program's by a relative error of at most 0.0036.
Values may be sent and summed in bfloat16 or wider, within the bound.
A program may use at most 64 MiB of HBM per device.

v0:
```python
import math

import jax
import jax.numpy as jnp
from jax import lax
from jax.sharding import PartitionSpec as P

HEADS = 16
HDIM = 128
TOP = 4
GROUP = 8


eps_norm = 1e-06


def for_sending(shard):

    def short(part):
        return part.astype(jnp.bfloat16) if part.dtype == jnp.float32 else part

    return jax.tree.map(short, shard)


def partner_2(block, axis, distance):
    count = lax.axis_size(axis)
    route = []
    for low in range(count):
        high = low | 1 << distance
        if high != low and high < count:
            route += [(low, high), (high, low)]
    return lax.ppermute(block, axis, route)


def route_slots(route_ids, expert_count):
    flat_ids = route_ids.reshape(-1)
    expert_iota = jnp.arange(expert_count, dtype=jnp.int32)
    one_hot = (flat_ids[:, None] == expert_iota[None, :]).astype(jnp.int32)
    earlier = jnp.cumsum(one_hot, axis=0) - one_hot
    slot_ids = jnp.sum(earlier * one_hot, axis=1)
    return (flat_ids, slot_ids)


def pack_slots(normed, flat_ids, slot_ids, expert_count, capacity):
    token_count = normed.shape[0]
    pair_tokens = jnp.arange(flat_ids.shape[0], dtype=jnp.int32) // TOP
    where_to = flat_ids * capacity + slot_ids
    source_row = (
        jnp.full((expert_count * capacity,), token_count, jnp.int32).at[where_to].set(pair_tokens)
    )
    padded = jnp.concatenate([normed, jnp.zeros((1, normed.shape[1]), normed.dtype)], axis=0)
    return padded[source_row].reshape(expert_count, capacity, normed.shape[1])


def attend_local(query, own_kv, own_cache, cache_count, group_kv, group_count):
    tok_count = query.shape[0]
    seg_rows = group_kv.shape[0] // GROUP
    prompt_ok = jnp.arange(GROUP * seg_rows, dtype=jnp.int32) % seg_rows < jnp.repeat(
        group_count, seg_rows
    )
    cache_ok = jnp.arange(own_cache.shape[0], dtype=jnp.int32) < cache_count
    fixed_ok = jnp.concatenate([prompt_ok, cache_ok])
    positions = jnp.arange(tok_count, dtype=jnp.int32)
    causal = positions[None, :] <= positions[:, None]
    visible = jnp.concatenate(
        [jnp.broadcast_to(fixed_ok[None, :], (tok_count, fixed_ok.shape[0])), causal], axis=1
    )
    keys_values = jnp.concatenate([group_kv, own_cache, own_kv], axis=0)
    model_width = query.shape[1]
    queries = query.reshape(tok_count, HEADS, HDIM)
    key_heads = keys_values[:, :model_width].reshape(-1, HEADS, HDIM)
    value_heads = keys_values[:, model_width:].reshape(-1, HEADS, HDIM)
    scores = jnp.einsum(
        "qhd,khd->hqk", queries, key_heads, preferred_element_type=jnp.float32
    ) / math.sqrt(HDIM)
    scores = jnp.where(visible[None], scores, -jnp.inf)
    row_peak = jnp.max(scores, axis=2, keepdims=True)
    weights = jnp.exp(scores - row_peak)
    totals = jnp.sum(weights, axis=2)
    rounded_probs = weights.astype(jnp.bfloat16)
    summed = jnp.einsum(
        "hqk,khd->qhd", rounded_probs, value_heads, preferred_element_type=jnp.float32
    )
    attended = summed / jnp.transpose(totals)[:, :, None]
    return attended.reshape(tok_count, model_width).astype(jnp.bfloat16)


def norm_rows(stream, gain_row):
    mean_sq = jnp.mean(stream * stream, axis=1, keepdims=True)
    return (stream * lax.rsqrt(mean_sq + eps_norm) * gain_row[None, :]).astype(jnp.bfloat16)


def activate(gate_up_out):
    half_width = gate_up_out.shape[-1] // 2
    return (jax.nn.silu(gate_up_out[..., :half_width]) * gate_up_out[..., half_width:]).astype(
        jnp.bfloat16
    )


def expert_local(arrived, rows_weight, cols_weight):
    flat_rows = arrived.reshape(-1, arrived.shape[-1])
    gate_up_out = jnp.dot(flat_rows, rows_weight, preferred_element_type=jnp.float32)
    activated = activate(gate_up_out)
    result = jnp.dot(activated, cols_weight, preferred_element_type=jnp.float32).astype(
        jnp.bfloat16
    )
    return result.reshape(arrived.shape)


def swap_level(gathered, bit_level, position):
    partner = jax.tree.map(
        lambda part, own: part.astype(own.dtype),
        partner_2(for_sending(gathered), "exp", bit_level),
        gathered,
    )
    is_upper = position // (1 << bit_level) % 2 == 1
    return tuple(
        (
            jnp.where(
                is_upper,
                jnp.concatenate([far_part, own_part]),
                jnp.concatenate([own_part, far_part]),
            )
            for own_part, far_part in zip(gathered, partner)
        )
    )


def body(
    new_q,
    new_kv,
    cache_kv,
    cache_len,
    prompt_kv,
    prompt_len,
    residual,
    norm_gain,
    routes,
    route_weight,
    gate_up,
    down_proj,
):
    gathered = (prompt_kv, prompt_len)
    position = lax.axis_index("exp")
    for bit_level in range(GROUP.bit_length() - 1):
        gathered = swap_level(gathered, bit_level, position)
    group_kv, group_count = gathered
    attended = attend_local(new_q, new_kv, cache_kv, cache_len[0], group_kv, group_count)
    stream = residual.astype(jnp.float32) + attended.astype(jnp.float32)
    normed = norm_rows(stream, norm_gain)
    experts_here = lax.axis_size("exp")
    token_count = new_q.shape[0]
    capacity = token_count * TOP * 5 // (4 * experts_here)
    flat_ids, slot_ids = route_slots(routes, experts_here)
    outbox = pack_slots(normed, flat_ids, slot_ids, experts_here, capacity)
    rows_weight, cols_weight = (
        lax.all_gather(gate_up[0], "req", axis=0, tiled=True),
        lax.all_gather(down_proj[0], "req", axis=1, tiled=True),
    )
    arrived = lax.all_to_all(outbox, "exp", split_axis=0, concat_axis=0, tiled=True)
    returned = lax.all_to_all(
        expert_local(arrived, rows_weight, cols_weight),
        "exp",
        split_axis=0,
        concat_axis=0,
        tiled=True,
    )
    model_width = returned.shape[-1]
    chosen = returned.reshape(-1, model_width)[flat_ids * capacity + slot_ids].astype(jnp.float32)
    chosen = chosen.reshape(token_count, TOP, model_width)
    combined = jnp.sum(chosen * route_weight[:, :, None], axis=1)
    return (stream + combined).astype(jnp.bfloat16)


def solution(mesh):
    return jax.shard_map(
        body,
        mesh=mesh,
        in_specs=(
            P(("req", "exp"), None),
            P(("req", "exp"), None),
            P(("req", "exp"), None),
            P(("req", "exp")),
            P(("req", "exp"), None),
            P(("req", "exp")),
            P(("req", "exp"), None),
            P(),
            P(("req", "exp"), None),
            P(("req", "exp"), None),
            P("exp", "req", None),
            P("exp", None, "req"),
        ),
        out_specs=P(("req", "exp"), None),
        check_vma=False,
    )
```

profile of v0, /device:TPU:32, one launch (start us, length us, event | category | flops | bytes accessed | tf_op | source)
XLA Modules:
  0.0 270.1 jit_solution(6271769204803086468)
XLA Ops:
  7.3 3.5 %collective-permute-start = (bf16[8,4096]{1,0:T(8,128)(2,1)}, bf16[8,4096]{1,0:T(8,128)(2,1)S(1)}, u32[]{:S(2)}, u32[]{:S(2)}) collective-permute-start(bf16[8,4096]{1,0:T(8,128)(2,1)} %param.16), channel_id=1, source_target_pairs={{0,1},{1,0},{2,3},{3,2},{4,5},{5,4},{6,7},{7,6},{8,9},{9,8},{10,11... | collective-permute-start | bytes 196616 | tf_op jit(solution)/shard_map/ppermute | solution.py:32
  10.8 2.4 collective-permute-start.3
  18.1 2.4 scatter_custom_fusion
  21.4 4.9 %collective-permute-start.4 = (s32[2]{0:T(128)S(1)}, s32[2]{0:T(128)S(1)}, u32[]{:S(2)}, u32[]{:S(2)}) collective-permute-start(s32[2]{0:T(128)S(1)} %broadcast_select_fusion), channel_id=1, source_target_pairs={{0,2},{2,0},{1,3},{3,1},{4,6},{6,4},{5,7},{7,5},{8,10},{10,8},{9,1... | collective-permute-start | bytes 32 | tf_op jit(solution)/shard_map/ppermute | solution.py:32
  26.3 2.0 collective-permute-done.4
  28.4 4.3 %collective-permute-start.5 = (s32[4]{0:T(128)S(1)}, s32[4]{0:T(128)S(1)}, u32[]{:S(2)}, u32[]{:S(2)}) collective-permute-start(s32[4]{0:T(128)S(1)} %broadcast_select_fusion.1), channel_id=1, source_target_pairs={{0,4},{4,0},{1,5},{5,1},{2,6},{6,2},{3,7},{7,3},{8,12},{12,8},{9,1... | collective-permute-start | bytes 56 | tf_op jit(solution)/shard_map/ppermute | solution.py:32
  35.3 4.9 %collective-permute-start.1 = (bf16[16,4096]{1,0:T(8,128)(2,1)S(1)}, bf16[16,4096]{1,0:T(8,128)(2,1)S(1)}, u32[]{:S(2)}, u32[]{:S(2)}) collective-permute-start(bf16[16,4096]{1,0:T(8,128)(2,1)S(1)} %maximum_select_fusion.2), channel_id=1, source_target_pairs={{0,2},{2,0},{1,3},{3,1},{4,6},{6,4},{5,7},{7,5},{8,10},{10,8},{9,1... | collective-permute-start | bytes 393224 | tf_op jit(solution)/shard_map/ppermute | solution.py:32
  40.3 3.4 %collective-permute-done.1 = bf16[16,4096]{1,0:T(8,128)(2,1)S(1)} collective-permute-done((bf16[16,4096]{1,0:T(8,128)(2,1)S(1)}, bf16[16,4096]{1,0:T(8,128)(2,1)S(1)}, u32[]{:S(2)}, u32[]{:S(2)}) %collective-permute-start.1) | collective-permute-done | bytes 131104 | tf_op jit(solution)/shard_map/ppermute | solution.py:32
  43.8 3.9 %collective-permute-start.2 = (bf16[32,4096]{1,0:T(8,128)(2,1)S(1)}, bf16[32,4096]{1,0:T(8,128)(2,1)S(1)}, u32[]{:S(2)}, u32[]{:S(2)}) collective-permute-start(bf16[32,4096]{1,0:T(8,128)(2,1)S(1)} %maximum_select_fusion.1), channel_id=1, source_target_pairs={{0,4},{4,0},{1,5},{5,1},{2,6},{6,2},{3,7},{7,3},{8,12},{12,8},{9,1... | collective-permute-start | bytes 786440 | tf_op jit(solution)/shard_map/ppermute | solution.py:32
  47.9 4.1 %collective-permute-done.2 = bf16[32,4096]{1,0:T(8,128)(2,1)S(1)} collective-permute-done((bf16[32,4096]{1,0:T(8,128)(2,1)S(1)}, bf16[32,4096]{1,0:T(8,128)(2,1)S(1)}, u32[]{:S(2)}, u32[]{:S(2)}) %collective-permute-start.2) | collective-permute-done | bytes 262176 | tf_op jit(solution)/shard_map/ppermute | solution.py:32
  57.3 4.1 %gather_fusion = bf16[640,2048]{1,0:T(8,128)(2,1)} fusion(bf16[129,2048]{1,0:T(8,128)(2,1)S(1)} %concatenate.63, s32[1024]{0:T(1024)S(1)} %pad_clamp_fusion.1), kind=kCustom, calls=%fused_computation | custom fusion | bytes 5245440 | tf_op jit(solution)/shard_map/gather | solution.py:52
  61.4 5.1 %reshape.97 = bf16[32,20,2048]{2,1,0:T(8,128)(2,1)} reshape(bf16[640,2048]{1,0:T(8,128)(2,1)} %gather_fusion) | data formatting | bytes 5242880 | tf_op jit(solution)/shard_map/reshape | solution.py:52
  66.5 12.9 %all-to-all-start = ((bf16[32,20,2048]{2,1,0:T(8,128)(2,1)}), bf16[32,20,2048]{2,1,0:T(8,128)(2,1)}, u32[]{:S(2)}, u32[]{:S(2)}) async-start(bf16[32,20,2048]{2,1,0:T(8,128)(2,1)} %reshape.97), calls=%async_computation | async-start | bytes 6291456 | tf_op jit(solution)/shard_map/all_to_all | solution.py:160
  80.2 69.2 %all-to-all-done = bf16[32,20,2048]{2,1,0:T(8,128)(2,1)} async-done(((bf16[32,20,2048]{2,1,0:T(8,128)(2,1)}), bf16[32,20,2048]{2,1,0:T(8,128)(2,1)}, u32[]{:S(2)}, u32[]{:S(2)}) %all-to-all-start) | async-done | bytes 2621472 | tf_op jit(solution)/shard_map/all_to_all | solution.py:160
  149.4 3.6 %reshape.98 = bf16[640,2048]{1,0:T(8,128)(2,1)S(1)} reshape(bf16[32,20,2048]{2,1,0:T(8,128)(2,1)} %all-to-all-done) | data formatting | bytes 5242880 | tf_op jit(solution)/shard_map/reshape | solution.py:101
  153.0 9.0 %fusion = f32[640,1536]{1,0:T(8,128)} fusion(bf16[640,2048]{1,0:T(8,128)(2,1)S(1)} %reshape.98, bf16[1,2048,1536]{2,1,0:T(8,128)(2,1)} %all-gather.5.cloned.1.call-done), kind=kOutput, calls=%fused_computation.3 | convolution fusion | flops 4026531840 | bytes 12845056 | tf_op jit(solution)/shard_map/dot_general | solution.py:102
  162.0 5.3 %convolution_convert_fusion = bf16[640,2048]{1,0:T(8,128)(2,1)S(1)} fusion(bf16[1,768,2048]{2,1,0:T(8,128)(2,1)} %all-gather.7.cloned.1.call-done, f32[640,1536]{1,0:T(8,128)} %fusion), kind=kOutput, calls=%fused_computation.6 | convolution fusion | flops 2017525760 | bytes 9699328 | tf_op jit(solution)/shard_map/dot_general | solution.py:104
  167.3 2.4 reshape.99
  169.7 5.3 %all-to-all-start.1 = ((bf16[32,20,2048]{2,1,0:T(8,128)(2,1)}), bf16[32,20,2048]{2,1,0:T(8,128)(2,1)}, u32[]{:S(2)}, u32[]{:S(2)}) async-start(bf16[32,20,2048]{2,1,0:T(8,128)(2,1)} %reshape.99), calls=%async_computation.1 | async-start | bytes 6291456 | tf_op jit(solution)/shard_map/all_to_all | solution.py:161
  175.2 69.8 %all-to-all-done.1 = bf16[32,20,2048]{2,1,0:T(8,128)(2,1)} async-done(((bf16[32,20,2048]{2,1,0:T(8,128)(2,1)}), bf16[32,20,2048]{2,1,0:T(8,128)(2,1)}, u32[]{:S(2)}, u32[]{:S(2)}) %all-to-all-start.1) | async-done | bytes 2621472 | tf_op jit(solution)/shard_map/all_to_all | solution.py:161
  245.0 3.6 %reshape.100 = bf16[640,2048]{1,0:T(8,128)(2,1)S(1)} reshape(bf16[32,20,2048]{2,1,0:T(8,128)(2,1)} %all-to-all-done.1) | data formatting | bytes 5242880 | tf_op jit(solution)/shard_map/reshape | solution.py:169
  248.6 3.3 %gather_fusion.1 = bf16[512,2048]{1,0:T(8,128)(2,1)} fusion(bf16[640,2048]{1,0:T(8,128)(2,1)S(1)} %reshape.100, s32[1024]{0:T(1024)S(1)} %pad_clamp_fusion), kind=kCustom, calls=%fused_computation.1 | custom fusion | bytes 4196352 | tf_op jit(solution)/shard_map/gather | solution.py:169
  251.9 4.8 %reshape.102 = f32[128,4,2048]{2,1,0:T(4,128)} reshape(bf16[512,2048]{1,0:T(8,128)(2,1)} %gather_fusion.1) | data formatting | bytes 6291456 | tf_op jit(solution)/shard_map/convert_element_type | solution.py:169
  256.7 5.5 %multiply_reduce_fusion = f32[128,2048]{1,0:T(8,128)S(1)} fusion(f32[128,4,2048]{2,1,0:T(4,128)} %reshape.102, f32[128,4]{1,0:T(8,128)S(1)} %copy.24), kind=kLoop, calls=%fused_computation.5 | loop fusion | flops 1835008 | bytes 5244928 | tf_op jit(solution)/shard_map/reduce_sum | solution.py:171
  (71 shorter events, 15.0 us)
Async XLA Ops:
  6.5 46.1 %copy-start = (bf16[128,2048]{1,0:T(8,128)(2,1)S(1)}, bf16[128,2048]{1,0:T(8,128)(2,1)}, u32[]{:S(2)}) copy-start(bf16[128,2048]{1,0:T(8,128)(2,1)} %param.12) | copy-start | bytes 1572868
  6.5 45.6 %copy-start.5 = (bf16[128,4096]{1,0:T(8,128)(2,1)S(1)}, bf16[128,4096]{1,0:T(8,128)(2,1)}, u32[]{:S(2)}) copy-start(bf16[128,4096]{1,0:T(8,128)(2,1)} %param.13) | copy-start | bytes 3145732
  6.5 45.6 %copy-start.6 = (bf16[128,4096]{1,0:T(8,128)(2,1)S(1)}, bf16[128,4096]{1,0:T(8,128)(2,1)}, u32[]{:S(2)}) copy-start(bf16[128,4096]{1,0:T(8,128)(2,1)} %param.14) | copy-start | bytes 3145732
  6.5 146.5 %all-gather.5.cloned.1.call-start = ((), (), s32[]{:S(2)}) async-start(), calls=%async_computation.2 | async-start | bytes 6684672 | tf_op jit(solution)/shard_map/all_gather | solution.py:157
  7.3 27.1 %collective-permute-start = (bf16[8,4096]{1,0:T(8,128)(2,1)}, bf16[8,4096]{1,0:T(8,128)(2,1)S(1)}, u32[]{:S(2)}, u32[]{:S(2)}) collective-permute-start(bf16[8,4096]{1,0:T(8,128)(2,1)} %param.16), channel_id=1, source_target_pairs={{0,1},{1,0},{2,3},{3,2},{4,5},{5,4},{6,7},{7,6},{8,9},{9,8},{10,11... | collective-permute-start | bytes 196616 | tf_op jit(solution)/shard_map/ppermute | solution.py:32
  10.8 9.8 %collective-permute-start.3 = (s32[1]{0:T(128)}, s32[1]{0:T(128)}, u32[]{:S(2)}, u32[]{:S(2)}) collective-permute-start(s32[1]{0:T(128)} %param.17), channel_id=1, source_target_pairs={{0,1},{1,0},{2,3},{3,2},{4,5},{5,4},{6,7},{7,6},{8,9},{9,8},{10,11... | collective-permute-start | bytes 20 | tf_op jit(solution)/shard_map/ppermute | solution.py:32
  21.4 6.9 %collective-permute-start.4 = (s32[2]{0:T(128)S(1)}, s32[2]{0:T(128)S(1)}, u32[]{:S(2)}, u32[]{:S(2)}) collective-permute-start(s32[2]{0:T(128)S(1)} %broadcast_select_fusion), channel_id=1, source_target_pairs={{0,2},{2,0},{1,3},{3,1},{4,6},{6,4},{5,7},{7,5},{8,10},{10,8},{9,1... | collective-permute-start | bytes 32 | tf_op jit(solution)/shard_map/ppermute | solution.py:32
  28.4 5.8 %collective-permute-start.5 = (s32[4]{0:T(128)S(1)}, s32[4]{0:T(128)S(1)}, u32[]{:S(2)}, u32[]{:S(2)}) collective-permute-start(s32[4]{0:T(128)S(1)} %broadcast_select_fusion.1), channel_id=1, source_target_pairs={{0,4},{4,0},{1,5},{5,1},{2,6},{6,2},{3,7},{7,3},{8,12},{12,8},{9,1... | collective-permute-start | bytes 56 | tf_op jit(solution)/shard_map/ppermute | solution.py:32
  35.3 8.4 %collective-permute-start.1 = (bf16[16,4096]{1,0:T(8,128)(2,1)S(1)}, bf16[16,4096]{1,0:T(8,128)(2,1)S(1)}, u32[]{:S(2)}, u32[]{:S(2)}) collective-permute-start(bf16[16,4096]{1,0:T(8,128)(2,1)S(1)} %maximum_select_fusion.2), channel_id=1, source_target_pairs={{0,2},{2,0},{1,3},{3,1},{4,6},{6,4},{5,7},{7,5},{8,10},{10,8},{9,1... | collective-permute-start | bytes 393224 | tf_op jit(solution)/shard_map/ppermute | solution.py:32
  43.8 8.3 %collective-permute-start.2 = (bf16[32,4096]{1,0:T(8,128)(2,1)S(1)}, bf16[32,4096]{1,0:T(8,128)(2,1)S(1)}, u32[]{:S(2)}, u32[]{:S(2)}) collective-permute-start(bf16[32,4096]{1,0:T(8,128)(2,1)S(1)} %maximum_select_fusion.1), channel_id=1, source_target_pairs={{0,4},{4,0},{1,5},{5,1},{2,6},{6,2},{3,7},{7,3},{8,12},{12,8},{9,1... | collective-permute-start | bytes 786440 | tf_op jit(solution)/shard_map/ppermute | solution.py:32
  55.0 1.1 copy-start.3
  55.0 2.1 copy-start.7
  56.1 1.0 copy-start.1
  66.5 82.8 %all-to-all-start = ((bf16[32,20,2048]{2,1,0:T(8,128)(2,1)}), bf16[32,20,2048]{2,1,0:T(8,128)(2,1)}, u32[]{:S(2)}, u32[]{:S(2)}) async-start(bf16[32,20,2048]{2,1,0:T(8,128)(2,1)} %reshape.97), calls=%async_computation | async-start | bytes 6291456 | tf_op jit(solution)/shard_map/all_to_all | solution.py:160
  79.4 82.6 %all-gather.7.cloned.1.call-start = ((), (), s32[]{:S(2)}) async-start(), calls=%async_computation.3 | async-start | bytes 3342336 | tf_op jit(solution)/shard_map/all_gather | solution.py:158
  169.7 5.3 %copy-start.8 = (f32[128,4]{0,1:T(4,128)S(1)}, f32[128,4]{0,1:T(4,128)}, u32[]{:S(2)}) copy-start(f32[128,4]{0,1:T(4,128)} %param.21) | copy-start | bytes 6148
  169.7 75.2 %all-to-all-start.1 = ((bf16[32,20,2048]{2,1,0:T(8,128)(2,1)}), bf16[32,20,2048]{2,1,0:T(8,128)(2,1)}, u32[]{:S(2)}, u32[]{:S(2)}) async-start(bf16[32,20,2048]{2,1,0:T(8,128)(2,1)} %reshape.99), calls=%async_computation.1 | async-start | bytes 6291456 | tf_op jit(solution)/shard_map/all_to_all | solution.py:161
  256.7 5.5 %copy-start.2 = (f32[128,2048]{1,0:T(8,128)S(1)}, f32[128,2048]{1,0:T(8,128)}, u32[]{:S(2)}) copy-start(f32[128,2048]{1,0:T(8,128)} %copy-done.1) | copy-start | bytes 3145732
  256.7 5.6 %copy-start.4 = (bf16[128,2048]{1,0:T(8,128)(2,1)S(1)}, bf16[128,2048]{1,0:T(8,128)(2,1)}, u32[]{:S(2)}) copy-start(bf16[128,2048]{1,0:T(8,128)(2,1)} %param.18) | copy-start | bytes 1572868
Sparse Core Ops, SparseCore 0:
  9.5 50.4 all-gather.4
  82.3 45.0 all-gather.6
where the time goes:
time: 271 us; the launch traced here: 270 us
  waiting for transfers between devices  151 us (56%)
  starting transfers between devices  42.4 us (16%)
  local copies, waits for them, and re-layouts  33.1 us (12%)
  matrix products  16.1 us (6%)
  between operations  15.1 us (6%)
  other arithmetic  12 us (4%)
    all_to_all x1, waiting for transfers between devices, body(): lax.all_to_all(expert_local(arrived, rows_weight, cols_weight), 'exp', sp...  69.8 us
    all_to_all x1, waiting for transfers between devices, body(): lax.all_to_all(outbox, 'exp', split_axis=0, concat_axis=0, tiled=True)  69.2 us
    ppermute x6, starting transfers between devices, partner_2(): return lax.ppermute(block, axis, route)  24 us
    all_to_all x1, starting transfers between devices, body(): lax.all_to_all(outbox, 'exp', split_axis=0, concat_axis=0, tiled=True)  12.9 us
    ppermute x6, waiting for transfers between devices, partner_2(): return lax.ppermute(block, axis, route)  11.1 us
    dot_general x1, matrix products, expert_local(): jnp.dot(flat_rows, rows_weight, preferred_element_type=jnp.float32)  9 us
    reduce_sum x1, other arithmetic, body(): combined = jnp.sum(chosen * route_weight[:, :, None], axis=1)  5.53 us
  transfers between devices with their start and end apart: 10, of which 6 were waited for; matrix products, arithmetic and copies ran while one was open for 13% of the time, Pallas kernels for 0%

commit v1 on v0

v1 whole, which is shorter than its diff:
```python
import math

import jax
import jax.numpy as jnp
from jax import lax
from jax.sharding import PartitionSpec as P

HEADS = 16
HDIM = 128
TOP = 4
GROUP = 8


eps_norm = 1e-06


HALVES = 2
SUB = 8


def gather_prompt(prompt_kv, prompt_len):
    rows = prompt_kv.shape[0]
    count_cols = jnp.broadcast_to(prompt_len.astype(jnp.bfloat16)[:, None], (rows, HDIM))
    block = jnp.concatenate([prompt_kv, count_cols], axis=1)
    axis_total = lax.axis_size("exp")
    parts = [block]
    for offset in range(1, GROUP):
        route = [(one, one ^ offset) for one in range(axis_total)]
        parts.append(lax.ppermute(block, "exp", route))
    gathered = jnp.concatenate(parts, axis=0)
    width = prompt_kv.shape[1]
    row_counts = gathered[:, width].astype(jnp.int32)
    row_index = jnp.arange(GROUP * rows, dtype=jnp.int32) % rows
    return gathered[:, :width], row_index < row_counts


def slot_layout(expert_count, capacity):
    main = capacity // SUB * SUB
    rest = capacity - main
    block = HALVES * capacity
    row = jnp.arange(expert_count * block, dtype=jnp.int32)
    expert = row // block
    inner = row % block
    in_main = inner < HALVES * main
    left_over = inner - HALVES * main
    half = jnp.where(in_main, inner // main, left_over // rest)
    slot = jnp.where(in_main, inner % main, main + left_over % rest)
    spread = (jnp.arange(expert_count, dtype=jnp.int32)[:, None] == expert[None, :]).astype(
        jnp.bfloat16
    )
    return spread, half, slot


def membership(routes, expert_count):
    experts = jnp.arange(expert_count, dtype=jnp.int32)
    return routes[:, :, None] == experts[None, None, :]


def slot_codes(chosen, spread):
    member = jnp.any(chosen, axis=1)
    tok_count = member.shape[0]
    order = jnp.arange(tok_count, dtype=jnp.int32)
    up_to = (order[None, :] <= order[:, None]).astype(jnp.bfloat16)
    upto_count = jnp.dot(
        up_to, member.astype(jnp.bfloat16), preferred_element_type=jnp.float32
    )
    codes = jnp.where(member, upto_count, 0.0).astype(jnp.bfloat16)
    return jnp.dot(codes, spread, preferred_element_type=jnp.float32).astype(jnp.bfloat16)


def pack_slots(normed, codes, half, slot):
    width = normed.shape[1] // HALVES
    wanted = (slot + 1).astype(jnp.bfloat16)
    picks = [
        jnp.where((half == which)[None, :] & (codes == wanted[None, :]), 1.0, 0.0).astype(
            jnp.bfloat16
        )
        for which in range(HALVES)
    ]
    stacked = jnp.concatenate(
        [normed[:, which * width : (which + 1) * width] for which in range(HALVES)], axis=0
    )
    return lax.dot_general(
        jnp.concatenate(picks, axis=0),
        stacked,
        (((0,), (0,)), ((), ())),
        preferred_element_type=jnp.float32,
    ).astype(jnp.bfloat16)


def combine_rows(returned, chosen, route_weight, codes, spread, half, slot):
    tok_count = route_weight.shape[0]
    by_expert = jnp.sum(jnp.where(chosen, route_weight[:, :, None], 0.0), axis=1)
    high = by_expert.astype(jnp.bfloat16)
    low = (by_expert - high.astype(jnp.float32)).astype(jnp.bfloat16)
    wide = jnp.dot(
        jnp.concatenate([high, low], axis=0), spread, preferred_element_type=jnp.float32
    ).astype(jnp.bfloat16)
    wanted = (slot + 1).astype(jnp.bfloat16)
    hit = codes == wanted[None, :]
    hits = jnp.concatenate([hit, hit], axis=0)
    mixes = [
        jnp.where((half == which)[None, :] & hits, wide, 0.0).astype(jnp.bfloat16)
        for which in range(HALVES)
    ]
    summed = jnp.dot(
        jnp.concatenate(mixes, axis=0), returned, preferred_element_type=jnp.float32
    )
    pieces = [
        summed[2 * which * tok_count : (2 * which + 1) * tok_count]
        + summed[(2 * which + 1) * tok_count : (2 * which + 2) * tok_count]
        for which in range(HALVES)
    ]
    return jnp.concatenate(pieces, axis=1)


def attend_local(query, own_kv, own_cache, cache_count, group_kv, prompt_ok):
    tok_count = query.shape[0]
    cache_ok = jnp.arange(own_cache.shape[0], dtype=jnp.int32) < cache_count
    fixed_ok = jnp.concatenate([prompt_ok, cache_ok])
    positions = jnp.arange(tok_count, dtype=jnp.int32)
    causal = positions[None, :] <= positions[:, None]
    visible = jnp.concatenate(
        [jnp.broadcast_to(fixed_ok[None, :], (tok_count, fixed_ok.shape[0])), causal], axis=1
    )
    keys_values = jnp.concatenate([group_kv, own_cache, own_kv], axis=0)
    model_width = query.shape[1]
    queries = query.reshape(tok_count, HEADS, HDIM)
    key_heads = keys_values[:, :model_width].reshape(-1, HEADS, HDIM)
    value_heads = keys_values[:, model_width:].reshape(-1, HEADS, HDIM)
    scores = jnp.einsum(
        "qhd,khd->hqk", queries, key_heads, preferred_element_type=jnp.float32
    ) / math.sqrt(HDIM)
    scores = jnp.where(visible[None], scores, -jnp.inf)
    row_peak = jnp.max(scores, axis=2, keepdims=True)
    weights = jnp.exp(scores - row_peak)
    totals = jnp.sum(weights, axis=2)
    rounded_probs = weights.astype(jnp.bfloat16)
    summed = jnp.einsum(
        "hqk,khd->qhd", rounded_probs, value_heads, preferred_element_type=jnp.float32
    )
    attended = summed / jnp.transpose(totals)[:, :, None]
    return attended.reshape(tok_count, model_width).astype(jnp.bfloat16)


def norm_rows(stream, gain_row):
    mean_sq = jnp.mean(stream * stream, axis=1, keepdims=True)
    return (stream * lax.rsqrt(mean_sq + eps_norm) * gain_row[None, :]).astype(jnp.bfloat16)


def activate(gate_up_out):
    half_width = gate_up_out.shape[-1] // 2
    return (jax.nn.silu(gate_up_out[..., :half_width]) * gate_up_out[..., half_width:]).astype(
        jnp.bfloat16
    )


def expert_local(arrived, rows_weight, cols_weight):
    sources, block, width = arrived.shape
    main = block // HALVES // SUB * SUB
    rest = block // HALVES - main
    tail = arrived[:, HALVES * main :]
    swapped = jnp.concatenate([tail[:, rest:], tail[:, :rest]], axis=1)
    left = jnp.concatenate([arrived[:, :main], tail], axis=1)
    right = jnp.concatenate([arrived[:, main : HALVES * main], swapped], axis=1)
    flat_rows = jnp.concatenate([left, right], axis=2).reshape(-1, HALVES * width)
    gate_up_out = jnp.dot(flat_rows, rows_weight, preferred_element_type=jnp.float32)
    activated = activate(gate_up_out)
    result = jnp.dot(activated, cols_weight, preferred_element_type=jnp.float32).astype(
        jnp.bfloat16
    )
    result = result.reshape(sources, main + HALVES * rest, HALVES * width)
    return jnp.concatenate(
        [
            result[:, :main, :width],
            result[:, :main, width:],
            result[:, main : main + rest, :width],
            result[:, main : main + rest, width:],
        ],
        axis=1,
    )


def body(
    new_q,
    new_kv,
    cache_kv,
    cache_len,
    prompt_kv,
    prompt_len,
    residual,
    norm_gain,
    routes,
    route_weight,
    gate_up,
    down_proj,
):
    group_kv, prompt_ok = gather_prompt(prompt_kv, prompt_len)
    experts_here = lax.axis_size("exp")
    token_count = new_q.shape[0]
    capacity = token_count * TOP * 5 // (4 * experts_here)
    spread, half, slot = slot_layout(experts_here, capacity)
    chosen = membership(routes, experts_here)
    codes = slot_codes(chosen, spread)
    rows_weight, cols_weight = (
        lax.all_gather(gate_up[0], "req", axis=0, tiled=True),
        lax.all_gather(down_proj[0], "req", axis=1, tiled=True),
    )
    attended = attend_local(new_q, new_kv, cache_kv, cache_len[0], group_kv, prompt_ok)
    stream = residual.astype(jnp.float32) + attended.astype(jnp.float32)
    normed = norm_rows(stream, norm_gain)
    outbox = pack_slots(normed, codes, half, slot)
    outbox = outbox.reshape(experts_here, HALVES * capacity, -1)
    arrived = lax.all_to_all(outbox, "exp", split_axis=0, concat_axis=0, tiled=True)
    returned = lax.all_to_all(
        expert_local(arrived, rows_weight, cols_weight),
        "exp",
        split_axis=0,
        concat_axis=0,
        tiled=True,
    )
    returned = returned.reshape(-1, returned.shape[-1])
    combined = combine_rows(returned, chosen, route_weight, codes, spread, half, slot)
    return (stream + combined).astype(jnp.bfloat16)


def solution(mesh):
    return jax.shard_map(
        body,
        mesh=mesh,
        in_specs=(
            P(("req", "exp"), None),
            P(("req", "exp"), None),
            P(("req", "exp"), None),
            P(("req", "exp")),
            P(("req", "exp"), None),
            P(("req", "exp")),
            P(("req", "exp"), None),
            P(),
            P(("req", "exp"), None),
            P(("req", "exp"), None),
            P("exp", "req", None),
            P("exp", None, "req"),
        ),
        out_specs=P(("req", "exp"), None),
        check_vma=False,
    )
```

time: 271 us -> 222 us (0.82)
  the two profiles are of different devices: /device:TPU:32 before, /device:TPU:58 now
where the time goes in v1:
time: 222 us
  waiting for transfers between devices  120 us (54%)
  starting transfers between devices  44.5 us (20%)
  matrix products  25.9 us (12%)
  between operations  15.1 us (7%)
  local copies, waits for them, and re-layouts  8.22 us (4%)
  other arithmetic  7.74 us (3%)
    all_to_all x1, waiting for transfers between devices, body(): lax.all_to_all(outbox, 'exp', split_axis=0, concat_axis=0, tiled=True)  57.6 us
    all_to_all x1, waiting for transfers between devices, body(): lax.all_to_all(expert_local(arrived, rows_weight, cols_weight), 'exp', sp...  57.2 us
    ppermute x7, starting transfers between devices, gather_prompt(): parts.append(lax.ppermute(block, 'exp', route))  24 us
    all_to_all x1, starting transfers between devices, body(): lax.all_to_all(outbox, 'exp', split_axis=0, concat_axis=0, tiled=True)  13.9 us
    dot_general x1, matrix products, expert_local(): jnp.dot(flat_rows, rows_weight, preferred_element_type=jnp.float32)  9.59 us
    all_to_all x1, starting transfers between devices, body(): lax.all_to_all(expert_local(arrived, rows_weight, cols_weight), 'exp', sp...  6.52 us
    dot_general x1, matrix products, expert_local(): jnp.dot(activated, cols_weight, preferred_element_type=jnp.float32)  5.95 us
  transfers between devices with their start and end apart: 11, of which 4 were waited for; matrix products, arithmetic and copies ran while one was open for 13% of the time, Pallas kernels for 0%

profile of v1, /device:TPU:58, one launch (start us, length us, event | category | flops | bytes accessed | tf_op | source)
XLA Modules:
  0.0 221.6 jit_solution(15147084586309573176)
XLA Ops:
  8.8 2.4 %collective-permute-start = (bf16[8,4224]{1,0:T(8,128)(2,1)S(1)}, bf16[8,4224]{1,0:T(8,128)(2,1)}, u32[]{:S(2)}, u32[]{:S(2)}) collective-permute-start(bf16[8,4224]{1,0:T(8,128)(2,1)S(1)} %get-tuple-element.25), channel_id=1, source_target_pairs={{0,1},{1,0},{2,3},{3,2},{4,5},{5,4},{6,7},{7,6},{8,9},{9,8},{10,11... | collective-permute-start | bytes 202760 | tf_op jit(solution)/shard_map/ppermute | solution.py:29
  11.2 4.3 %collective-permute-start.1 = (bf16[8,4224]{1,0:T(8,128)(2,1)S(1)}, bf16[8,4224]{1,0:T(8,128)(2,1)S(1)}, u32[]{:S(2)}, u32[]{:S(2)}) collective-permute-start(bf16[8,4224]{1,0:T(8,128)(2,1)S(1)} %get-tuple-element.25), channel_id=1, source_target_pairs={{0,2},{1,3},{2,0},{3,1},{4,6},{5,7},{6,4},{7,5},{8,10},{9,11},{10,... | collective-permute-start | bytes 202760 | tf_op jit(solution)/shard_map/ppermute | solution.py:29
  15.6 2.4 %collective-permute-start.2 = (bf16[8,4224]{1,0:T(8,128)(2,1)S(1)}, bf16[8,4224]{1,0:T(8,128)(2,1)S(1)}, u32[]{:S(2)}, u32[]{:S(2)}) collective-permute-start(bf16[8,4224]{1,0:T(8,128)(2,1)S(1)} %get-tuple-element.25), channel_id=1, source_target_pairs={{0,3},{1,2},{2,1},{3,0},{4,7},{5,6},{6,5},{7,4},{8,11},{9,10},{10,... | collective-permute-start | bytes 202760 | tf_op jit(solution)/shard_map/ppermute | solution.py:29
  18.0 4.3 %collective-permute-start.3 = (bf16[8,4224]{1,0:T(8,128)(2,1)S(1)}, bf16[8,4224]{1,0:T(8,128)(2,1)S(1)}, u32[]{:S(2)}, u32[]{:S(2)}) collective-permute-start(bf16[8,4224]{1,0:T(8,128)(2,1)S(1)} %get-tuple-element.25), channel_id=1, source_target_pairs={{0,4},{1,5},{2,6},{3,7},{4,0},{5,1},{6,2},{7,3},{8,12},{9,13},{10,... | collective-permute-start | bytes 202760 | tf_op jit(solution)/shard_map/ppermute | solution.py:29
  22.3 3.1 %collective-permute-start.4 = (bf16[8,4224]{1,0:T(8,128)(2,1)S(1)}, bf16[8,4224]{1,0:T(8,128)(2,1)S(1)}, u32[]{:S(2)}, u32[]{:S(2)}) collective-permute-start(bf16[8,4224]{1,0:T(8,128)(2,1)S(1)} %get-tuple-element.25), channel_id=1, source_target_pairs={{0,5},{1,4},{2,7},{3,6},{4,1},{5,0},{6,3},{7,2},{8,13},{9,12},{10,... | collective-permute-start | bytes 202760 | tf_op jit(solution)/shard_map/ppermute | solution.py:29
  26.8 1.4 select_convert_fusion.1
  28.3 4.6 %collective-permute-start.5 = (bf16[8,4224]{1,0:T(8,128)(2,1)S(1)}, bf16[8,4224]{1,0:T(8,128)(2,1)S(1)}, u32[]{:S(2)}, u32[]{:S(2)}) collective-permute-start(bf16[8,4224]{1,0:T(8,128)(2,1)S(1)} %get-tuple-element.25), channel_id=1, source_target_pairs={{0,6},{1,7},{2,4},{3,5},{4,2},{5,3},{6,0},{7,1},{8,14},{9,15},{10,... | collective-permute-start | bytes 202760 | tf_op jit(solution)/shard_map/ppermute | solution.py:29
  33.7 2.9 %collective-permute-start.6 = (bf16[8,4224]{1,0:T(8,128)(2,1)S(1)}, bf16[8,4224]{1,0:T(8,128)(2,1)S(1)}, u32[]{:S(2)}, u32[]{:S(2)}) collective-permute-start(bf16[8,4224]{1,0:T(8,128)(2,1)S(1)} %get-tuple-element.25), channel_id=1, source_target_pairs={{0,7},{1,6},{2,5},{3,4},{4,3},{5,2},{6,1},{7,0},{8,15},{9,14},{10,... | collective-permute-start | bytes 202760 | tf_op jit(solution)/shard_map/ppermute | solution.py:29
  36.9 4.0 %collective-permute-done.6 = bf16[8,4224]{1,0:T(8,128)(2,1)S(1)} collective-permute-done((bf16[8,4224]{1,0:T(8,128)(2,1)S(1)}, bf16[8,4224]{1,0:T(8,128)(2,1)S(1)}, u32[]{:S(2)}, u32[]{:S(2)}) %collective-permute-start.6) | collective-permute-done | bytes 67616 | tf_op jit(solution)/shard_map/ppermute | solution.py:29
  42.9 1.2 fusion.23
  46.2 2.3 %convolution_convert_fusion = bf16[1280,1024]{1,0:T(8,128)(2,1)} fusion(bf16[128,1280]{1,0:T(8,128)(2,1)S(1)} %copy-done.8, bf16[128,1280]{1,0:T(8,128)(2,1)S(1)} %copy-done.7, bf16[128,1024]{1,0:T(8,128)(2,1)S(1)} %get-tuple-element.22, bf16[128,1024]{1,0:T(8,128)(2,1)S(1)} %get-tuple-element.21), kind=kOutput, calls=%fused_computation.2 | convolution fusion | flops 674758656 | bytes 3801088 | tf_op jit(solution)/shard_map/dot_general | solution.py:83
  48.6 13.9 %all-to-all-start = ((bf16[32,40,1024]{2,1,0:T(8,128)(2,1)}), bf16[32,40,1024]{2,1,0:T(8,128)(2,1)}, u32[]{:S(2)}, u32[]{:S(2)}) async-start(bf16[32,40,1024]{2,1,0:T(8,128)(2,1)} %bitcast.61), calls=%async_computation | async-start | bytes 5242880 | tf_op jit(solution)/shard_map/all_to_all | solution.py:214
  63.2 57.6 %all-to-all-done = bf16[32,40,1024]{2,1,0:T(8,128)(2,1)} async-done(((bf16[32,40,1024]{2,1,0:T(8,128)(2,1)}), bf16[32,40,1024]{2,1,0:T(8,128)(2,1)}, u32[]{:S(2)}, u32[]{:S(2)}) %all-to-all-start) | async-done | bytes 2621472 | tf_op jit(solution)/shard_map/all_to_all | solution.py:214
  120.7 1.1 slice.93
  121.8 1.4 fusion.76
  123.2 1.7 fusion.75
  125.0 2.2 maximum_maximum_fusion
  127.1 9.6 %fusion = f32[768,1536]{1,0:T(8,128)} fusion(bf16[768,2048]{1,0:T(8,128)(2,1)} %bitcast.60, bf16[1,2048,1536]{2,1,0:T(8,128)(2,1)} %all-gather.5.cloned.1.call-done), kind=kOutput, calls=%fused_computation | convolution fusion | flops 4831838208 | bytes 14155776 | tf_op jit(solution)/shard_map/dot_general | solution.py:167
  136.7 6.0 %convolution_convert_fusion.1 = bf16[768,2048]{1,0:T(8,128)(2,1)S(1)} fusion(bf16[1,768,2048]{2,1,0:T(8,128)(2,1)} %all-gather.7.cloned.1.call-done, f32[768,1536]{1,0:T(8,128)} %fusion), kind=kOutput, calls=%fused_computation.3 | convolution fusion | flops 2421030912 | bytes 11010048 | tf_op jit(solution)/shard_map/dot_general | solution.py:169
  143.1 2.0 pad_maximum_fusion.1
  145.0 6.5 %all-to-all-start.1 = ((bf16[32,40,1024]{2,1,0:T(8,128)(2,1)}), bf16[32,40,1024]{2,1,0:T(8,128)(2,1)}, u32[]{:S(2)}, u32[]{:S(2)}) async-start(bf16[32,40,1024]{2,1,0:T(8,128)(2,1)} %pad_maximum_fusion.1), calls=%async_computation.1 | async-start | bytes 5242880 | tf_op jit(solution)/shard_map/all_to_all | solution.py:215
  151.6 1.5 and_select_fusion.1
  153.1 57.2 %all-to-all-done.1 = bf16[32,40,1024]{2,1,0:T(8,128)(2,1)} async-done(((bf16[32,40,1024]{2,1,0:T(8,128)(2,1)}), bf16[32,40,1024]{2,1,0:T(8,128)(2,1)}, u32[]{:S(2)}, u32[]{:S(2)}) %all-to-all-start.1) | async-done | bytes 2621472 | tf_op jit(solution)/shard_map/all_to_all | solution.py:215
  210.3 3.3 %fusion.15 = f32[512,1024]{1,0:T(8,128)S(1)} fusion(bf16[1280,1024]{1,0:T(8,128)(2,1)} %bitcast.11, bf16[256,1280]{1,0:T(8,128)(2,1)S(1)} %get-tuple-element.20, bf16[256,1280]{1,0:T(8,128)(2,1)S(1)} %get-tuple-element.19), kind=kOutput, calls=%fused_computation.27 | convolution fusion | flops 1344798720 | bytes 6029312 | tf_op jit(solution)/shard_map/dot_general | solution.py:106
  (65 shorter events, 9.8 us)
Async XLA Ops:
  6.5 35.2 %copy-start = (bf16[128,2048]{1,0:T(8,128)(2,1)S(1)}, bf16[128,2048]{1,0:T(8,128)(2,1)}, u32[]{:S(2)}) copy-start(bf16[128,2048]{1,0:T(8,128)(2,1)} %param.12) | copy-start | bytes 1572868
  6.5 34.7 %copy-start.2 = (bf16[128,4096]{1,0:T(8,128)(2,1)S(1)}, bf16[128,4096]{1,0:T(8,128)(2,1)}, u32[]{:S(2)}) copy-start(bf16[128,4096]{1,0:T(8,128)(2,1)} %param.13) | copy-start | bytes 3145732
  6.5 34.7 %copy-start.3 = (bf16[128,4096]{1,0:T(8,128)(2,1)S(1)}, bf16[128,4096]{1,0:T(8,128)(2,1)}, u32[]{:S(2)}) copy-start(bf16[128,4096]{1,0:T(8,128)(2,1)} %param.14) | copy-start | bytes 3145732
  6.5 120.6 %all-gather.5.cloned.1.call-start = ((), (), s32[]{:S(2)}) async-start(), calls=%async_computation.2 | async-start | bytes 6684672 | tf_op jit(solution)/shard_map/all_gather | solution.py:206
  8.8 19.5 %collective-permute-start = (bf16[8,4224]{1,0:T(8,128)(2,1)S(1)}, bf16[8,4224]{1,0:T(8,128)(2,1)}, u32[]{:S(2)}, u32[]{:S(2)}) collective-permute-start(bf16[8,4224]{1,0:T(8,128)(2,1)S(1)} %get-tuple-element.25), channel_id=1, source_target_pairs={{0,1},{1,0},{2,3},{3,2},{4,5},{5,4},{6,7},{7,6},{8,9},{9,8},{10,11... | collective-permute-start | bytes 202760 | tf_op jit(solution)/shard_map/ppermute | solution.py:29
  11.2 22.5 %collective-permute-start.1 = (bf16[8,4224]{1,0:T(8,128)(2,1)S(1)}, bf16[8,4224]{1,0:T(8,128)(2,1)S(1)}, u32[]{:S(2)}, u32[]{:S(2)}) collective-permute-start(bf16[8,4224]{1,0:T(8,128)(2,1)S(1)} %get-tuple-element.25), channel_id=1, source_target_pairs={{0,2},{1,3},{2,0},{3,1},{4,6},{5,7},{6,4},{7,5},{8,10},{9,11},{10,... | collective-permute-start | bytes 202760 | tf_op jit(solution)/shard_map/ppermute | solution.py:29
  15.6 21.1 %collective-permute-start.2 = (bf16[8,4224]{1,0:T(8,128)(2,1)S(1)}, bf16[8,4224]{1,0:T(8,128)(2,1)S(1)}, u32[]{:S(2)}, u32[]{:S(2)}) collective-permute-start(bf16[8,4224]{1,0:T(8,128)(2,1)S(1)} %get-tuple-element.25), channel_id=1, source_target_pairs={{0,3},{1,2},{2,1},{3,0},{4,7},{5,6},{6,5},{7,4},{8,11},{9,10},{10,... | collective-permute-start | bytes 202760 | tf_op jit(solution)/shard_map/ppermute | solution.py:29
  18.0 18.7 %collective-permute-start.3 = (bf16[8,4224]{1,0:T(8,128)(2,1)S(1)}, bf16[8,4224]{1,0:T(8,128)(2,1)S(1)}, u32[]{:S(2)}, u32[]{:S(2)}) collective-permute-start(bf16[8,4224]{1,0:T(8,128)(2,1)S(1)} %get-tuple-element.25), channel_id=1, source_target_pairs={{0,4},{1,5},{2,6},{3,7},{4,0},{5,1},{6,2},{7,3},{8,12},{9,13},{10,... | collective-permute-start | bytes 202760 | tf_op jit(solution)/shard_map/ppermute | solution.py:29
  22.3 14.4 %collective-permute-start.4 = (bf16[8,4224]{1,0:T(8,128)(2,1)S(1)}, bf16[8,4224]{1,0:T(8,128)(2,1)S(1)}, u32[]{:S(2)}, u32[]{:S(2)}) collective-permute-start(bf16[8,4224]{1,0:T(8,128)(2,1)S(1)} %get-tuple-element.25), channel_id=1, source_target_pairs={{0,5},{1,4},{2,7},{3,6},{4,1},{5,0},{6,3},{7,2},{8,13},{9,12},{10,... | collective-permute-start | bytes 202760 | tf_op jit(solution)/shard_map/ppermute | solution.py:29
  28.3 8.6 %collective-permute-start.5 = (bf16[8,4224]{1,0:T(8,128)(2,1)S(1)}, bf16[8,4224]{1,0:T(8,128)(2,1)S(1)}, u32[]{:S(2)}, u32[]{:S(2)}) collective-permute-start(bf16[8,4224]{1,0:T(8,128)(2,1)S(1)} %get-tuple-element.25), channel_id=1, source_target_pairs={{0,6},{1,7},{2,4},{3,5},{4,2},{5,3},{6,0},{7,1},{8,14},{9,15},{10,... | collective-permute-start | bytes 202760 | tf_op jit(solution)/shard_map/ppermute | solution.py:29
  33.7 7.1 %collective-permute-start.6 = (bf16[8,4224]{1,0:T(8,128)(2,1)S(1)}, bf16[8,4224]{1,0:T(8,128)(2,1)S(1)}, u32[]{:S(2)}, u32[]{:S(2)}) collective-permute-start(bf16[8,4224]{1,0:T(8,128)(2,1)S(1)} %get-tuple-element.25), channel_id=1, source_target_pairs={{0,7},{1,6},{2,5},{3,4},{4,3},{5,2},{6,1},{7,0},{8,15},{9,14},{10,... | collective-permute-start | bytes 202760 | tf_op jit(solution)/shard_map/ppermute | solution.py:29
  44.1 1.0 copy-start.1
  44.1 1.3 copy-start.4
  45.1 1.0 copy-start.7
  45.1 1.1 copy-start.8
  48.6 72.2 %all-to-all-start = ((bf16[32,40,1024]{2,1,0:T(8,128)(2,1)}), bf16[32,40,1024]{2,1,0:T(8,128)(2,1)}, u32[]{:S(2)}, u32[]{:S(2)}) async-start(bf16[32,40,1024]{2,1,0:T(8,128)(2,1)} %bitcast.61), calls=%async_computation | async-start | bytes 5242880 | tf_op jit(solution)/shard_map/all_to_all | solution.py:214
  62.4 74.3 %all-gather.7.cloned.1.call-start = ((), (), s32[]{:S(2)}) async-start(), calls=%async_computation.3 | async-start | bytes 3342336 | tf_op jit(solution)/shard_map/all_gather | solution.py:207
  145.0 6.5 %copy-start.5 = (s32[128,4]{0,1:T(4,128)S(1)}, s32[128,4]{0,1:T(4,128)}, u32[]{:S(2)}) copy-start(s32[128,4]{0,1:T(4,128)} %param.20) | copy-start | bytes 6148
  145.0 6.5 %copy-start.6 = (f32[128,4]{0,1:T(4,128)S(1)}, f32[128,4]{0,1:T(4,128)}, u32[]{:S(2)}) copy-start(f32[128,4]{0,1:T(4,128)} %param.21) | copy-start | bytes 6148
  145.0 65.2 %all-to-all-start.1 = ((bf16[32,40,1024]{2,1,0:T(8,128)(2,1)}), bf16[32,40,1024]{2,1,0:T(8,128)(2,1)}, u32[]{:S(2)}, u32[]{:S(2)}) async-start(bf16[32,40,1024]{2,1,0:T(8,128)(2,1)} %pad_maximum_fusion.1), calls=%async_computation.1 | async-start | bytes 5242880 | tf_op jit(solution)/shard_map/all_to_all | solution.py:215
Sparse Core Ops, SparseCore 0:
  9.5 51.5 all-gather.4
  65.3 47.3 all-gather.6

commit v2 on v1

v2 whole, which is shorter than its diff:
```python
import math

import jax
import jax.numpy as jnp
import numpy as np
from jax import lax
from jax.experimental import pallas as pl
from jax.experimental.pallas import tpu as pltpu
from jax.sharding import PartitionSpec as P

HEADS = 16
HDIM = 128
TOP = 4
GROUP = 8


eps_norm = 1e-06


HALVES = 2
SUB = 8


def slot_layout(expert_count, capacity):
    main = capacity // SUB * SUB
    rest = capacity - main
    block = HALVES * capacity
    row = jnp.arange(expert_count * block, dtype=jnp.int32)
    expert = row // block
    inner = row % block
    in_main = inner < HALVES * main
    left_over = inner - HALVES * main
    half = jnp.where(in_main, inner // main, left_over // rest)
    slot = jnp.where(in_main, inner % main, main + left_over % rest)
    spread = (jnp.arange(expert_count, dtype=jnp.int32)[:, None] == expert[None, :]).astype(
        jnp.bfloat16
    )
    return spread, half, slot


def membership(routes, expert_count):
    experts = jnp.arange(expert_count, dtype=jnp.int32)
    return routes[:, :, None] == experts[None, None, :]


def slot_codes(chosen, spread):
    member = jnp.any(chosen, axis=1)
    tok_count = member.shape[0]
    order = jnp.arange(tok_count, dtype=jnp.int32)
    up_to = (order[None, :] <= order[:, None]).astype(jnp.bfloat16)
    upto_count = jnp.dot(
        up_to, member.astype(jnp.bfloat16), preferred_element_type=jnp.float32
    )
    codes = jnp.where(member, upto_count, 0.0).astype(jnp.bfloat16)
    return jnp.dot(codes, spread, preferred_element_type=jnp.float32).astype(jnp.bfloat16)


def combine_rows(returned, chosen, route_weight, codes, spread, half, slot):
    tok_count = route_weight.shape[0]
    by_expert = jnp.sum(jnp.where(chosen, route_weight[:, :, None], 0.0), axis=1)
    high = by_expert.astype(jnp.bfloat16)
    low = (by_expert - high.astype(jnp.float32)).astype(jnp.bfloat16)
    wide = jnp.dot(
        jnp.concatenate([high, low], axis=0), spread, preferred_element_type=jnp.float32
    ).astype(jnp.bfloat16)
    wanted = (slot + 1).astype(jnp.bfloat16)
    hit = codes == wanted[None, :]
    hits = jnp.concatenate([hit, hit], axis=0)
    mixes = [
        jnp.where((half == which)[None, :] & hits, wide, 0.0).astype(jnp.bfloat16)
        for which in range(HALVES)
    ]
    summed = jnp.dot(
        jnp.concatenate(mixes, axis=0), returned, preferred_element_type=jnp.float32
    )
    pieces = [
        summed[2 * which * tok_count : (2 * which + 1) * tok_count]
        + summed[(2 * which + 1) * tok_count : (2 * which + 2) * tok_count]
        for which in range(HALVES)
    ]
    return jnp.concatenate(pieces, axis=1)


def slot_tables(expert_count, capacity):
    main = capacity // SUB * SUB
    rest = capacity - main
    block = HALVES * capacity
    row = np.arange(expert_count * block)
    inner = row % block
    in_main = inner < HALVES * main
    left_over = inner - HALVES * main
    half = np.where(in_main, inner // main, left_over // rest)
    slot = np.where(in_main, inner % main, main + left_over % rest)
    spread = (np.arange(expert_count)[None, :] == (row // block)[:, None]).astype(np.float32)
    wanted = np.stack(
        [np.where(half == which, slot + 1, -1) for which in range(HALVES)], axis=1
    ).astype(np.float32)
    return spread, wanted


NT = (((1,), (1,)), ((), ()))


def attend_kernel(
    count_ref,
    query_ref,
    own_ref,
    cache_ref,
    block_ref,
    residual_ref,
    gain_ref,
    routes_ref,
    spread_ref,
    wanted_ref,
    stream_ref,
    outbox_ref,
    far_ref,
    local_ref,
    send_sem,
    recv_sem,
):
    tok_count, width = query_ref.shape
    heads = width // HDIM
    experts = spread_ref.shape[1]
    position = lax.axis_index("exp")
    base = position // GROUP * GROUP
    rank = position - base
    barrier = pltpu.get_barrier_semaphore()
    for offset in range(1, GROUP):
        pl.semaphore_signal(
            barrier,
            inc=1,
            device_id={"exp": base + (rank + offset) % GROUP},
            device_id_type=pl.DeviceIdType.MESH,
        )
    pl.semaphore_wait(barrier, GROUP - 1)
    copies = []
    for offset in range(1, GROUP):
        copy = pltpu.make_async_remote_copy(
            src_ref=block_ref,
            dst_ref=far_ref.at[offset - 1],
            send_sem=send_sem.at[offset - 1],
            recv_sem=recv_sem.at[offset - 1],
            device_id={"exp": base + (rank + offset) % GROUP},
            device_id_type=pl.DeviceIdType.MESH,
        )
        copy.start()
        copies.append(copy)

    scale = 1.0 / math.sqrt(HDIM)
    rows = lax.broadcasted_iota(jnp.int32, (tok_count, tok_count), 0)
    cols = lax.broadcasted_iota(jnp.int32, (tok_count, tok_count), 1)
    causal = cols <= rows
    live = lax.broadcasted_iota(jnp.int32, (tok_count, cache_ref.shape[0]), 1) < count_ref[0]
    peaks = []
    sums = []
    for head in range(heads):
        at = slice(head * HDIM, (head + 1) * HDIM)
        values_at = slice(width + head * HDIM, width + (head + 1) * HDIM)
        query = query_ref[:, at]
        own = lax.dot_general(query, own_ref[:, at], NT, preferred_element_type=jnp.float32)
        old = lax.dot_general(query, cache_ref[:, at], NT, preferred_element_type=jnp.float32)
        own = jnp.where(causal, own * scale, -jnp.inf)
        old = jnp.where(live, old * scale, -jnp.inf)
        peak = jnp.max(jnp.maximum(own, old), axis=1, keepdims=True)
        own = jnp.exp(own - peak)
        old = jnp.exp(old - peak)
        sums.append(jnp.sum(own + old, axis=1, keepdims=True))
        peaks.append(peak)
        local_ref[:, at] = jnp.dot(
            own.astype(jnp.bfloat16), own_ref[:, values_at], preferred_element_type=jnp.float32
        ) + jnp.dot(
            old.astype(jnp.bfloat16), cache_ref[:, values_at], preferred_element_type=jnp.float32
        )

    lanes = lax.broadcasted_iota(jnp.int32, (tok_count, experts), 1)
    member = jnp.zeros((tok_count, experts), jnp.float32)
    for k in range(TOP):
        member = member + jnp.where(routes_ref[:, k : k + 1] == lanes, 1.0, 0.0)
    ranks = jnp.dot(
        jnp.where(causal, 1.0, 0.0).astype(jnp.bfloat16),
        member.astype(jnp.bfloat16),
        preferred_element_type=jnp.float32,
    )
    codes = (ranks * member).astype(jnp.bfloat16)
    codes = lax.dot_general(spread_ref[...], codes, NT, preferred_element_type=jnp.float32)
    picks = [
        jnp.where(codes == wanted_ref[:, which : which + 1], 1.0, 0.0).astype(jnp.bfloat16)
        for which in range(HALVES)
    ]

    for copy in copies:
        copy.wait()
    prompt_rows = block_ref.shape[0]
    far = jnp.concatenate([block_ref[...][None], far_ref[...]], axis=0)
    in_segment = lax.broadcasted_iota(jnp.int32, (GROUP, prompt_rows, HDIM), 1)
    dead = jnp.where(
        in_segment.astype(jnp.float32) < far[:, :, 2 * width :].astype(jnp.float32), 0.0, 1.0
    )
    keys_total = GROUP * prompt_rows
    dead = dead.reshape(keys_total, HDIM).astype(jnp.bfloat16)
    far = far.reshape(keys_total, far.shape[2])
    ones = jnp.full((tok_count, HDIM), 1.0 / HDIM, jnp.bfloat16)
    hidden = lax.dot_general(ones, dead, NT, preferred_element_type=jnp.float32) > 0.5
    squares = jnp.zeros((tok_count, HDIM), jnp.float32)
    for head in range(heads):
        at = slice(head * HDIM, (head + 1) * HDIM)
        values_at = slice(width + head * HDIM, width + (head + 1) * HDIM)
        scores = lax.dot_general(
            query_ref[:, at], far[:, at], NT, preferred_element_type=jnp.float32
        )
        scores = jnp.where(hidden, -jnp.inf, scores * scale)
        peak = jnp.maximum(peaks[head], jnp.max(scores, axis=1, keepdims=True))
        shrink = jnp.exp(peaks[head] - peak)
        weights = jnp.exp(scores - peak)
        total = sums[head] * shrink + jnp.sum(weights, axis=1, keepdims=True)
        summed = local_ref[:, at] * shrink + jnp.dot(
            weights.astype(jnp.bfloat16), far[:, values_at], preferred_element_type=jnp.float32
        )
        attended = (summed / total).astype(jnp.bfloat16).astype(jnp.float32)
        stream = residual_ref[:, at].astype(jnp.float32) + attended
        stream_ref[:, at] = stream
        squares = squares + stream * stream
    mean_sq = jnp.sum(squares, axis=1, keepdims=True) / width
    normed = (stream_ref[...] * lax.rsqrt(mean_sq + eps_norm) * gain_ref[...]).astype(jnp.bfloat16)
    part = width // HALVES
    outbox_ref[...] = (
        jnp.dot(picks[0], normed[:, :part], preferred_element_type=jnp.float32)
        + jnp.dot(picks[1], normed[:, part:], preferred_element_type=jnp.float32)
    ).astype(jnp.bfloat16)


def attend_and_pack(
    query, own_kv, own_cache, cache_count, prompt_kv, prompt_len, residual, gain, routes, experts, capacity
):
    tok_count, width = query.shape
    prompt_rows = prompt_kv.shape[0]
    count_cols = jnp.broadcast_to(prompt_len.astype(jnp.bfloat16)[:, None], (prompt_rows, HDIM))
    block = jnp.concatenate([prompt_kv, count_cols], axis=1)
    spread, wanted = slot_tables(experts, capacity)
    vmem = pl.BlockSpec(memory_space=pltpu.VMEM)
    slots = experts * HALVES * capacity
    return pl.pallas_call(
        attend_kernel,
        out_shape=(
            jax.ShapeDtypeStruct((tok_count, width), jnp.float32),
            jax.ShapeDtypeStruct((slots, width // HALVES), jnp.bfloat16),
        ),
        in_specs=[pl.BlockSpec(memory_space=pltpu.SMEM)] + [vmem] * 9,
        out_specs=(vmem, vmem),
        scratch_shapes=[
            pltpu.VMEM((GROUP - 1,) + block.shape, jnp.bfloat16),
            pltpu.VMEM((tok_count, width), jnp.float32),
            pltpu.SemaphoreType.DMA((GROUP - 1,)),
            pltpu.SemaphoreType.DMA((GROUP - 1,)),
        ],
        compiler_params=pltpu.CompilerParams(
            collective_id=0, has_side_effects=True, vmem_limit_bytes=40 * 1024 * 1024
        ),
        cost_estimate=pl.CostEstimate(
            flops=2 * 10**9, bytes_accessed=8 * 10**6, transcendentals=655360
        ),
    )(
        cache_count,
        query,
        own_kv,
        own_cache,
        block,
        residual,
        gain[None, :],
        routes,
        jnp.asarray(spread, jnp.bfloat16),
        jnp.asarray(wanted),
    )


def expert_kernel(arrived_ref, gate_ref, up_ref, down_ref, out_ref, rows_ref, total_ref):
    step = pl.program_id(0)
    sources, block, width = arrived_ref.shape
    main = block // HALVES // SUB * SUB
    rest = block // HALVES - main
    tall = sources * main

    @pl.when(step == 0)
    def _():
        rows_ref[:tall, :width] = arrived_ref[:, :main, :].reshape(tall, width)
        rows_ref[:tall, width:] = arrived_ref[:, main : HALVES * main, :].reshape(tall, width)
        tail = arrived_ref[:, HALVES * main :, :].astype(jnp.float32)
        swapped = jnp.concatenate([tail[:, rest:], tail[:, :rest]], axis=1)
        rows_ref[tall:, :width] = tail.reshape(-1, width).astype(jnp.bfloat16)
        rows_ref[tall:, width:] = swapped.reshape(-1, width).astype(jnp.bfloat16)

    rows = rows_ref[...]
    gate = jnp.dot(rows, gate_ref[...], preferred_element_type=jnp.float32)
    up = jnp.dot(rows, up_ref[...], preferred_element_type=jnp.float32)
    activated = (gate / (1.0 + jnp.exp(-gate)) * up).astype(jnp.bfloat16)
    result = jnp.dot(activated, down_ref[...], preferred_element_type=jnp.float32)

    @pl.when(step == 0)
    def _():
        total_ref[...] = result

    @pl.when(step > 0)
    def _():
        total_ref[...] = total_ref[...] + result

    @pl.when(step == pl.num_programs(0) - 1)
    def _():
        out_ref[:, :main, :] = (
            total_ref[:tall, :width].astype(jnp.bfloat16).reshape(sources, main, width)
        )
        out_ref[:, main : HALVES * main, :] = (
            total_ref[:tall, width:].astype(jnp.bfloat16).reshape(sources, main, width)
        )
        left = total_ref[tall:, :width].reshape(sources, HALVES * rest, width)
        right = total_ref[tall:, width:].reshape(sources, HALVES * rest, width)
        out_ref[:, HALVES * main :, :] = jnp.concatenate(
            [left[:, :rest], right[:, :rest]], axis=1
        ).astype(jnp.bfloat16)


def expert_local(arrived, rows_weight, cols_weight):
    sources, block, width = arrived.shape
    main = block // HALVES // SUB * SUB
    rest = block // HALVES - main
    row_total = sources * (main + HALVES * rest)
    depth, both = rows_weight.shape
    hidden = both // 2
    tile = 256
    steps = hidden // tile
    whole = pl.BlockSpec(arrived.shape, lambda j: (0, 0, 0))
    return pl.pallas_call(
        expert_kernel,
        grid=(steps,),
        out_shape=jax.ShapeDtypeStruct(arrived.shape, jnp.bfloat16),
        in_specs=[
            whole,
            pl.BlockSpec((depth, tile), lambda j: (0, j)),
            pl.BlockSpec((depth, tile), lambda j: (0, steps + j)),
            pl.BlockSpec((tile, depth), lambda j: (j, 0)),
        ],
        out_specs=whole,
        scratch_shapes=[
            pltpu.VMEM((row_total, depth), jnp.bfloat16),
            pltpu.VMEM((row_total, depth), jnp.float32),
        ],
        compiler_params=pltpu.CompilerParams(vmem_limit_bytes=48 * 1024 * 1024),
        cost_estimate=pl.CostEstimate(
            flops=7 * 10**9, bytes_accessed=15 * 10**6, transcendentals=589824
        ),
    )(arrived, rows_weight, rows_weight, cols_weight)


def body(
    new_q,
    new_kv,
    cache_kv,
    cache_len,
    prompt_kv,
    prompt_len,
    residual,
    norm_gain,
    routes,
    route_weight,
    gate_up,
    down_proj,
):
    experts_here = lax.axis_size("exp")
    token_count = new_q.shape[0]
    capacity = token_count * TOP * 5 // (4 * experts_here)
    spread, half, slot = slot_layout(experts_here, capacity)
    chosen = membership(routes, experts_here)
    codes = slot_codes(chosen, spread)
    rows_weight, cols_weight = (
        lax.all_gather(gate_up[0], "req", axis=0, tiled=True),
        lax.all_gather(down_proj[0], "req", axis=1, tiled=True),
    )
    stream, outbox = attend_and_pack(
        new_q,
        new_kv,
        cache_kv,
        cache_len,
        prompt_kv,
        prompt_len,
        residual,
        norm_gain,
        routes,
        experts_here,
        capacity,
    )
    outbox = outbox.reshape(experts_here, HALVES * capacity, -1)
    arrived = lax.all_to_all(outbox, "exp", split_axis=0, concat_axis=0, tiled=True)
    returned = lax.all_to_all(
        expert_local(arrived, rows_weight, cols_weight),
        "exp",
        split_axis=0,
        concat_axis=0,
        tiled=True,
    )
    returned = returned.reshape(-1, returned.shape[-1])
    combined = combine_rows(returned, chosen, route_weight, codes, spread, half, slot)
    return (stream + combined).astype(jnp.bfloat16)


def solution(mesh):
    return jax.shard_map(
        body,
        mesh=mesh,
        in_specs=(
            P(("req", "exp"), None),
            P(("req", "exp"), None),
            P(("req", "exp"), None),
            P(("req", "exp")),
            P(("req", "exp"), None),
            P(("req", "exp")),
            P(("req", "exp"), None),
            P(),
            P(("req", "exp"), None),
            P(("req", "exp"), None),
            P("exp", "req", None),
            P("exp", None, "req"),
        ),
        out_specs=P(("req", "exp"), None),
        check_vma=False,
    )
```

time: 222 us -> 209 us (0.941)
  the two profiles are of different devices: /device:TPU:58 before, /device:TPU:8 now
where the time goes in v2:
time: 209 us; the launch traced here: 208 us
  blocking collectives  73.3 us (35%)
  waiting for transfers between devices  63.2 us (30%)
  Pallas kernels  29.8 us (14%)
  between operations  14.8 us (7%)
  local copies, waits for them, and re-layouts  11 us (5%)
  starting transfers between devices  10.4 us (5%)
  matrix products  4.38 us (2%)
    all_to_all x1, blocking collectives, body(): lax.all_to_all(outbox, 'exp', split_axis=0, concat_axis=0, tiled=True)  73.3 us
    all_to_all x1, waiting for transfers between devices, body(): lax.all_to_all(expert_local(arrived, rows_weight, cols_weight), 'exp', sp...  59.7 us
    pallas_call x1, Pallas kernels, attend_and_pack(): pl.pallas_call(attend_kernel, out_shape=(jax.ShapeDtypeStruct((tok_count,...  16.4 us
    pallas_call x1, Pallas kernels, expert_local(): pl.pallas_call(expert_kernel, grid=(steps,), out_shape=jax.ShapeDtypeStru...  13.4 us
    all_to_all x1, starting transfers between devices, body(): lax.all_to_all(expert_local(arrived, rows_weight, cols_weight), 'exp', sp...  10.3 us
    unnamed x23, local copies, waits for them, and re-layouts  10.1 us
  transfers between devices with their start and end apart: 3, of which 2 were waited for; matrix products, arithmetic and copies ran while one was open for 2% of the time, Pallas kernels for 8%

profile of v2, /device:TPU:8, one launch (start us, length us, event | category | flops | bytes accessed | tf_op | source)
XLA Modules:
  0.0 208.1 jit_solution(18049586454913858214)
XLA Ops:
  6.5 0.7 all-gather.7.cloned.1.call-update
  7.3 0.7 all-gather.5.cloned.1.call-update
  9.3 0.8 copy.21.routes_ref
  10.1 0.8 concatenate.15.block_ref
  10.9 1.2 copy-done.2
  12.2 1.2 copy-done.3
  13.4 1.0 copy-done.4
  14.4 1.0 copy-done.5
  15.5 0.7 copy-done.6
  16.2 1.1 copy-done.7
  17.3 1.0 copy-done.8
  18.2 16.4 %shard_map.136 = (f32[128,2048]{1,0:T(8,128)S(1)}, bf16[1280,1024]{1,0:T(8,128)(2,1)S(1)}) custom-call(s32[1]{0:T(128)S(6)} %copy.24.count_ref, bf16[128,2048]{1,0:T(8,128)(2,1)S(1)} %copy-done.4, bf16[128,4096]{1,0:T(8,128)(2,1)S(1)} %copy-done.2, bf16[128,4096]{1,0:T(8,128)(2,1)S(1)} %copy-done.3, bf16[8,4224]{1,0:T(8,128)(2,1)S(1)} %concatenate.15.block_ref, ...), custom_call_target="tpu_custom_call" | custom-call | flops 2000000000 | bytes 8000000 | tf_op jit(solution)/shard_map/pallas_call | solution.py:243
  34.6 1.0 copy-done
  35.7 73.3 %all_to_all.10.arrived_ref = bf16[32,40,1024]{2,1,0:T(8,128)(2,1)S(1)} all-to-all(bf16[32,40,1024]{2,1,0:T(8,128)(2,1)S(1)} %bitcast.8), channel_id=1, replica_groups=mesh['req'=16,'exp'=32] {'exp'}, dimensions={0} | all-to-all | bytes 5242880 | tf_op jit(solution)/shard_map/all_to_all | solution.py:392
  109.0 2.1 %all-gather.5.cloned.1.call-done = bf16[1,2048,1536]{2,1,0:T(8,128)(2,1)} async-done(((bf16[1,128,1536]{2,1,0:T(8,128)(2,1)}), bf16[1,2048,1536]{2,1,0:T(8,128)(2,1)}) %all-gather.5.cloned.1.call-update) | async-done | bytes 6291472 | tf_op jit(solution)/shard_map/all_gather | solution.py:375
  111.1 13.4 %shard_map.137 = bf16[32,40,1024]{2,1,0:T(8,128)(2,1)} custom-call(bf16[32,40,1024]{2,1,0:T(8,128)(2,1)S(1)} %all_to_all.10.arrived_ref, bf16[2048,1536]{1,0:T(8,128)(2,1)} %bitcast.11, bf16[2048,1536]{1,0:T(8,128)(2,1)} %bitcast.12, bf16[768,2048]{1,0:T(8,128)(2,1)} %bitcast.13), custom_call_target="tpu_custom_call" | custom-call | flops 7000000000 | bytes 15000000 | tf_op jit(solution)/shard_map/pallas_call | solution.py:332
  124.5 10.3 %all-to-all-start.1 = ((bf16[32,40,1024]{2,1,0:T(8,128)(2,1)}), bf16[32,40,1024]{2,1,0:T(8,128)(2,1)S(1)}, u32[]{:S(2)}, u32[]{:S(2)}) async-start(bf16[32,40,1024]{2,1,0:T(8,128)(2,1)} %shard_map.137), calls=%async_computation.1 | async-start | bytes 5242880 | tf_op jit(solution)/shard_map/all_to_all | solution.py:393
  135.0 0.4 fusion
  135.4 1.3 and_select_fusion.1
  136.8 59.7 %all-to-all-done.1 = bf16[32,40,1024]{2,1,0:T(8,128)(2,1)S(1)} async-done(((bf16[32,40,1024]{2,1,0:T(8,128)(2,1)}), bf16[32,40,1024]{2,1,0:T(8,128)(2,1)S(1)}, u32[]{:S(2)}, u32[]{:S(2)}) %all-to-all-start.1) | async-done | bytes 2621472 | tf_op jit(solution)/shard_map/all_to_all | solution.py:393
  196.5 2.6 %fusion.1 = f32[512,1024]{1,0:T(8,128)S(1)} fusion(bf16[1280,1024]{1,0:T(8,128)(2,1)S(1)} %bitcast.10, bf16[256,1280]{1,0:T(8,128)(2,1)} %get-tuple-element.14, bf16[256,1280]{1,0:T(8,128)(2,1)S(1)} %get-tuple-element.13), kind=kOutput, calls=%fused_computation.3 | convolution fusion | flops 1344798720 | bytes 6029312 | tf_op jit(solution)/shard_map/dot_general | solution.py:73
  199.1 0.2 slice_add_fusion.1
  199.3 1.0 copy-done.1
  200.3 0.9 fusion.6
  (21 shorter events, 0.1 us)
Async XLA Ops:
  6.5 102.5 %all-gather.7.cloned.1.call-start = ((), (), s32[]{:S(2)}) async-start(), calls=%async_computation.3 | async-start | bytes 3342336 | tf_op jit(solution)/shard_map/all_gather | solution.py:376
  7.3 103.9 %all-gather.5.cloned.1.call-start = ((), (), s32[]{:S(2)}) async-start(), calls=%async_computation.2 | async-start | bytes 6684672 | tf_op jit(solution)/shard_map/all_gather | solution.py:375
  10.9 1.2 copy-start.2
  12.2 1.2 copy-start.3
  13.4 1.0 copy-start.4
  14.4 1.0 copy-start.5
  15.5 0.7 copy-start.6
  16.2 1.1 copy-start.7
  17.3 1.0 copy-start.8
  34.6 1.0 copy-start
  124.5 10.4 %copy-start.9 = (s32[128,4]{0,1:T(4,128)S(1)}, s32[128,4]{0,1:T(4,128)}, u32[]{:S(2)}) copy-start(s32[128,4]{0,1:T(4,128)} %param.22) | copy-start | bytes 6148
  124.5 10.4 %copy-start.10 = (f32[128,4]{0,1:T(4,128)S(1)}, f32[128,4]{0,1:T(4,128)}, u32[]{:S(2)}) copy-start(f32[128,4]{0,1:T(4,128)} %param.23) | copy-start | bytes 6148
  124.5 71.9 %all-to-all-start.1 = ((bf16[32,40,1024]{2,1,0:T(8,128)(2,1)}), bf16[32,40,1024]{2,1,0:T(8,128)(2,1)S(1)}, u32[]{:S(2)}, u32[]{:S(2)}) async-start(bf16[32,40,1024]{2,1,0:T(8,128)(2,1)} %shard_map.137), calls=%async_computation.1 | async-start | bytes 5242880 | tf_op jit(solution)/shard_map/all_to_all | solution.py:393
  199.1 1.2 copy-start.1
Sparse Core Ops, SparseCore 0:
  9.4 51.7 all-gather.6
  63.3 47.7 all-gather.4

commit v3 on v2

--- a/solution.py
+++ b/solution.py
@@ -103,22 +103,44 @@
 
 def attend_kernel(
     count_ref,
+    block_ref,
+    routes_ref,
+    query_hbm,
+    own_hbm,
+    cache_hbm,
+    residual_hbm,
+    gain_hbm,
+    spread_hbm,
+    wanted_hbm,
+    stream_hbm,
+    outbox_ref,
     query_ref,
     own_ref,
     cache_ref,
-    block_ref,
     residual_ref,
     gain_ref,
-    routes_ref,
     spread_ref,
     wanted_ref,
     stream_ref,
-    outbox_ref,
     far_ref,
     local_ref,
+    load_sem,
     send_sem,
     recv_sem,
 ):
+    loads = []
+    for source, target in (
+        (query_hbm, query_ref),
+        (own_hbm, own_ref),
+        (cache_hbm, cache_ref),
+        (spread_hbm, spread_ref),
+        (wanted_hbm, wanted_ref),
+        (residual_hbm, residual_ref),
+        (gain_hbm, gain_ref),
+    ):
+        load = pltpu.make_async_copy(source, target, load_sem.at[len(loads)])
+        load.start()
+        loads.append(load)
     tok_count, width = query_ref.shape
     heads = width // HDIM
     experts = spread_ref.shape[1]
@@ -154,6 +176,8 @@
     live = lax.broadcasted_iota(jnp.int32, (tok_count, cache_ref.shape[0]), 1) < count_ref[0]
     peaks = []
     sums = []
+    for load in loads[:3]:
+        load.wait()
     for head in range(heads):
         at = slice(head * HDIM, (head + 1) * HDIM)
         values_at = slice(width + head * HDIM, width + (head + 1) * HDIM)
@@ -173,17 +197,19 @@
             old.astype(jnp.bfloat16), cache_ref[:, values_at], preferred_element_type=jnp.float32
         )
 
-    lanes = lax.broadcasted_iota(jnp.int32, (tok_count, experts), 1)
-    member = jnp.zeros((tok_count, experts), jnp.float32)
+    for load in loads[3:]:
+        load.wait()
+    names = lax.broadcasted_iota(jnp.int32, (experts, tok_count), 0)
+    member = jnp.zeros((experts, tok_count), jnp.float32)
     for k in range(TOP):
-        member = member + jnp.where(routes_ref[:, k : k + 1] == lanes, 1.0, 0.0)
+        member = member + jnp.where(routes_ref[k : k + 1, :] == names, 1.0, 0.0)
     ranks = jnp.dot(
-        jnp.where(causal, 1.0, 0.0).astype(jnp.bfloat16),
         member.astype(jnp.bfloat16),
+        jnp.where(rows <= cols, 1.0, 0.0).astype(jnp.bfloat16),
         preferred_element_type=jnp.float32,
     )
     codes = (ranks * member).astype(jnp.bfloat16)
-    codes = lax.dot_general(spread_ref[...], codes, NT, preferred_element_type=jnp.float32)
+    codes = jnp.dot(spread_ref[...], codes, preferred_element_type=jnp.float32)
     picks = [
         jnp.where(codes == wanted_ref[:, which : which + 1], 1.0, 0.0).astype(jnp.bfloat16)
         for which in range(HALVES)
@@ -223,11 +249,14 @@
         squares = squares + stream * stream
     mean_sq = jnp.sum(squares, axis=1, keepdims=True) / width
     normed = (stream_ref[...] * lax.rsqrt(mean_sq + eps_norm) * gain_ref[...]).astype(jnp.bfloat16)
+    store = pltpu.make_async_copy(stream_ref, stream_hbm, load_sem.at[len(loads)])
+    store.start()
     part = width // HALVES
     outbox_ref[...] = (
         jnp.dot(picks[0], normed[:, :part], preferred_element_type=jnp.float32)
         + jnp.dot(picks[1], normed[:, part:], preferred_element_type=jnp.float32)
     ).astype(jnp.bfloat16)
+    store.wait()
 
 
 def attend_and_pack(
@@ -239,6 +268,7 @@
     block = jnp.concatenate([prompt_kv, count_cols], axis=1)
     spread, wanted = slot_tables(experts, capacity)
     vmem = pl.BlockSpec(memory_space=pltpu.VMEM)
+    outside = pl.BlockSpec(memory_space=pltpu.HBM)
     slots = experts * HALVES * capacity
     return pl.pallas_call(
         attend_kernel,
@@ -246,29 +276,38 @@
             jax.ShapeDtypeStruct((tok_count, width), jnp.float32),
             jax.ShapeDtypeStruct((slots, width // HALVES), jnp.bfloat16),
         ),
-        in_specs=[pl.BlockSpec(memory_space=pltpu.SMEM)] + [vmem] * 9,
-        out_specs=(vmem, vmem),
+        in_specs=[pl.BlockSpec(memory_space=pltpu.SMEM)] + [vmem] * 2 + [outside] * 7,
+        out_specs=(outside, vmem),
         scratch_shapes=[
+            pltpu.VMEM(query.shape, query.dtype),
+            pltpu.VMEM(own_kv.shape, own_kv.dtype),
+            pltpu.VMEM(own_cache.shape, own_cache.dtype),
+            pltpu.VMEM(residual.shape, residual.dtype),
+            pltpu.VMEM((1, width), jnp.float32),
+            pltpu.VMEM(spread.shape, jnp.bfloat16),
+            pltpu.VMEM(wanted.shape, jnp.float32),
+            pltpu.VMEM((tok_count, width), jnp.float32),
             pltpu.VMEM((GROUP - 1,) + block.shape, jnp.bfloat16),
             pltpu.VMEM((tok_count, width), jnp.float32),
+            pltpu.SemaphoreType.DMA((8,)),
             pltpu.SemaphoreType.DMA((GROUP - 1,)),
             pltpu.SemaphoreType.DMA((GROUP - 1,)),
         ],
         compiler_params=pltpu.CompilerParams(
-            collective_id=0, has_side_effects=True, vmem_limit_bytes=40 * 1024 * 1024
+            collective_id=0, has_side_effects=True, vmem_limit_bytes=63 * 1024 * 1024
         ),
         cost_estimate=pl.CostEstimate(
             flops=2 * 10**9, bytes_accessed=8 * 10**6, transcendentals=655360
         ),
     )(
         cache_count,
+        block,
+        routes.T,
         query,
         own_kv,
         own_cache,
-        block,
         residual,
         gain[None, :],
-        routes,
         jnp.asarray(spread, jnp.bfloat16),
         jnp.asarray(wanted),
     )
@@ -294,7 +333,8 @@
     gate = jnp.dot(rows, gate_ref[...], preferred_element_type=jnp.float32)
     up = jnp.dot(rows, up_ref[...], preferred_element_type=jnp.float32)
     activated = (gate / (1.0 + jnp.exp(-gate)) * up).astype(jnp.bfloat16)
-    result = jnp.dot(activated, down_ref[...], preferred_element_type=jnp.float32)
+    down = jnp.concatenate([down_ref[n] for n in range(down_ref.shape[0])], axis=1)
+    result = jnp.dot(activated, down, preferred_element_type=jnp.float32)
 
     @pl.when(step == 0)
     def _():
@@ -337,7 +377,7 @@
             whole,
             pl.BlockSpec((depth, tile), lambda j: (0, j)),
             pl.BlockSpec((depth, tile), lambda j: (0, steps + j)),
-            pl.BlockSpec((tile, depth), lambda j: (j, 0)),
+            pl.BlockSpec((cols_weight.shape[0], tile, cols_weight.shape[2]), lambda j: (0, j, 0)),
         ],
         out_specs=whole,
         scratch_shapes=[
@@ -373,7 +413,7 @@
     codes = slot_codes(chosen, spread)
     rows_weight, cols_weight = (
         lax.all_gather(gate_up[0], "req", axis=0, tiled=True),
-        lax.all_gather(down_proj[0], "req", axis=1, tiled=True),
+        lax.all_gather(down_proj, "req", axis=0, tiled=True),
     )
     stream, outbox = attend_and_pack(
         new_q,

time: 209 us -> 204 us (0.976)
  local copies, waits for them, and re-layouts: 11 us -> 2.52 us
  Pallas kernels: 29.8 us -> 32.2 us
    unnamed x23 -> x6, local copies, waits for them, and re-layouts: 10.1 us -> 1.04 us
    pallas_call x1, Pallas kernels: 16.4 us -> 18.8 us  [attend_and_pack(): pl.pallas_call(attend_kernel, out_shape=(jax.ShapeDtypeStruct((tok_count,...]
  transfers between devices with their start and end apart: 3 -> 3, of which waited for: 2 -> 2; matrix products, arithmetic and copies ran while one was open for 2% -> 2% of each run, Pallas kernels for 8% -> 9%
where the time goes in v3:
time: 204 us
  blocking collectives  73.5 us (36%)
  waiting for transfers between devices  65 us (32%)
  Pallas kernels  32.2 us (16%)
  between operations  14.8 us (7%)
  starting transfers between devices  10.4 us (5%)
  matrix products  4.37 us (2%)
  local copies, waits for them, and re-layouts  2.52 us (1%)
    all_to_all x1, blocking collectives, body(): lax.all_to_all(outbox, 'exp', split_axis=0, concat_axis=0, tiled=True)  73.5 us
    all_to_all x1, waiting for transfers between devices, body(): lax.all_to_all(expert_local(arrived, rows_weight, cols_weight), 'exp', sp...  59.7 us
    pallas_call x1, Pallas kernels, attend_and_pack(): pl.pallas_call(attend_kernel, out_shape=(jax.ShapeDtypeStruct((tok_count,...  18.8 us
    pallas_call x1, Pallas kernels, expert_local(): pl.pallas_call(expert_kernel, grid=(steps,), out_shape=jax.ShapeDtypeStru...  13.4 us
    all_to_all x1, starting transfers between devices, body(): lax.all_to_all(expert_local(arrived, rows_weight, cols_weight), 'exp', sp...  10.3 us
  transfers between devices with their start and end apart: 3, of which 2 were waited for; matrix products, arithmetic and copies ran while one was open for 2% of the time, Pallas kernels for 9%

profile of v3, /device:TPU:8, one launch (start us, length us, event | category | flops | bytes accessed | tf_op | source)
XLA Modules:
  0.0 203.9 jit_solution(5710458351483405594)
XLA Ops:
  6.5 0.0 all-gather.4.cloned.1.call-start
  6.5 0.7 all-gather.4.cloned.1.call-update
  7.3 0.0 all-gather.6.cloned.1.call-start
  7.3 0.7 all-gather.6.cloned.1.call-update
  9.3 1.5 concatenate.15.block_ref
  10.8 18.8 %shard_map.136 = (f32[128,2048]{1,0:T(8,128)}, bf16[1280,1024]{1,0:T(8,128)(2,1)}) custom-call(s32[1]{0:T(128)S(6)} %copy.21.count_ref, bf16[8,4224]{1,0:T(8,128)(2,1)} %concatenate.15.block_ref, s32[4,128]{1,0:T(4,128)} %bitcast.10, bf16[128,2048]{1,0:T(8,128)(2,1)} %query_hbm.1, bf16[128,4096]{1,0:T(8,128)(2,1)} %own_hbm.1, bf16[128,4096]{1,0:T(8,128)(2,1)} %cache_hbm.1, ...), custom_call_target="tpu_custom_call" | custom-call | flops 2000000000 | bytes 8000000 | tf_op jit(solution)/shard_map/pallas_call | solution.py:273
  29.6 73.5 %all_to_all.10.arrived_ref = bf16[32,40,1024]{2,1,0:T(8,128)(2,1)S(1)} all-to-all(bf16[32,40,1024]{2,1,0:T(8,128)(2,1)} %bitcast.9), channel_id=1, replica_groups=mesh['req'=16,'exp'=32] {'exp'}, dimensions={0} | all-to-all | bytes 5242880 | tf_op jit(solution)/shard_map/all_to_all | solution.py:432
  103.0 0.0 all-gather.4.cloned.1.call-done.down_ref
  103.0 3.9 %all-gather.6.cloned.1.call-done = bf16[1,2048,1536]{2,1,0:T(8,128)(2,1)} async-done(((bf16[1,128,1536]{2,1,0:T(8,128)(2,1)}), bf16[1,2048,1536]{2,1,0:T(8,128)(2,1)}) %all-gather.6.cloned.1.call-update) | async-done | bytes 6291472 | tf_op jit(solution)/shard_map/all_gather | solution.py:415
  106.9 13.4 %shard_map.137 = bf16[32,40,1024]{2,1,0:T(8,128)(2,1)} custom-call(bf16[32,40,1024]{2,1,0:T(8,128)(2,1)S(1)} %all_to_all.10.arrived_ref, bf16[2048,1536]{1,0:T(8,128)(2,1)} %bitcast.11, bf16[2048,1536]{1,0:T(8,128)(2,1)} %bitcast.12, bf16[16,768,128]{2,1,0:T(8,128)(2,1)} %all-gather.4.cloned.1.call-done.down_ref), custom_call_target="tpu_custom_call" | custom-call | flops 7000000000 | bytes 15000000 | tf_op jit(solution)/shard_map/pallas_call | solution.py:372
  120.4 0.0 copy-start.1
  120.4 0.0 copy-start.2
  120.4 10.3 %all-to-all-start.1 = ((bf16[32,40,1024]{2,1,0:T(8,128)(2,1)}), bf16[32,40,1024]{2,1,0:T(8,128)(2,1)S(1)}, u32[]{:S(2)}, u32[]{:S(2)}) async-start(bf16[32,40,1024]{2,1,0:T(8,128)(2,1)} %shard_map.137), calls=%async_computation.1 | async-start | bytes 5242880 | tf_op jit(solution)/shard_map/all_to_all | solution.py:433
  130.7 0.0 copy-done.1
  130.8 0.0 copy-done.2
  130.8 0.4 fusion
  131.3 1.3 and_select_fusion.1
  132.6 59.7 %all-to-all-done.1 = bf16[32,40,1024]{2,1,0:T(8,128)(2,1)S(1)} async-done(((bf16[32,40,1024]{2,1,0:T(8,128)(2,1)}), bf16[32,40,1024]{2,1,0:T(8,128)(2,1)S(1)}, u32[]{:S(2)}, u32[]{:S(2)}) %all-to-all-start.1) | async-done | bytes 2621472 | tf_op jit(solution)/shard_map/all_to_all | solution.py:433
  192.3 2.6 %fusion.1 = f32[512,1024]{1,0:T(8,128)S(1)} fusion(bf16[1280,1024]{1,0:T(8,128)(2,1)S(1)} %bitcast.8, bf16[256,1280]{1,0:T(8,128)(2,1)} %get-tuple-element.14, bf16[256,1280]{1,0:T(8,128)(2,1)S(1)} %get-tuple-element.13), kind=kOutput, calls=%fused_computation.3 | convolution fusion | flops 1344798720 | bytes 6029312 | tf_op jit(solution)/shard_map/dot_general | solution.py:73
  194.9 0.0 copy-start
  194.9 0.2 slice_add_fusion.1
  195.1 1.0 copy-done
  196.1 0.9 fusion.6
  (5 shorter events, 0.1 us)
Async XLA Ops:
  6.5 96.5 %all-gather.4.cloned.1.call-start = ((), (), s32[]{:S(2)}) async-start(), calls=%async_computation.2 | async-start | bytes 3342336 | tf_op jit(solution)/shard_map/all_gather | solution.py:416
  7.3 99.7 %all-gather.6.cloned.1.call-start = ((), (), s32[]{:S(2)}) async-start(), calls=%async_computation.3 | async-start | bytes 6684672 | tf_op jit(solution)/shard_map/all_gather | solution.py:415
  120.4 10.4 %copy-start.1 = (s32[128,4]{0,1:T(4,128)S(1)}, s32[128,4]{0,1:T(4,128)}, u32[]{:S(2)}) copy-start(s32[128,4]{0,1:T(4,128)} %param.22) | copy-start | bytes 6148
  120.4 10.4 %copy-start.2 = (f32[128,4]{0,1:T(4,128)S(1)}, f32[128,4]{0,1:T(4,128)}, u32[]{:S(2)}) copy-start(f32[128,4]{0,1:T(4,128)} %param.23) | copy-start | bytes 6148
  120.4 71.9 %all-to-all-start.1 = ((bf16[32,40,1024]{2,1,0:T(8,128)(2,1)}), bf16[32,40,1024]{2,1,0:T(8,128)(2,1)S(1)}, u32[]{:S(2)}, u32[]{:S(2)}) async-start(bf16[32,40,1024]{2,1,0:T(8,128)(2,1)} %shard_map.137), calls=%async_computation.1 | async-start | bytes 5242880 | tf_op jit(solution)/shard_map/all_to_all | solution.py:433
  194.9 1.2 copy-start
Sparse Core Ops, SparseCore 0:
  9.5 47.8 all-gather.3
  59.5 47.4 all-gather.5

commit v4 on v3

--- a/solution.py
+++ b/solution.py
@@ -19,6 +19,7 @@
 
 HALVES = 2
 SUB = 8
+ACROSS = 4
 
 
 def slot_layout(expert_count, capacity):
@@ -313,82 +314,173 @@
     )
 
 
-def expert_kernel(arrived_ref, gate_ref, up_ref, down_ref, out_ref, rows_ref, total_ref):
-    step = pl.program_id(0)
-    sources, block, width = arrived_ref.shape
+def pack_weights(gate_up, down_proj):
+    hidden = down_proj.shape[0]
+    pieces = gate_up.shape[1] // HDIM
+    tall = hidden // pieces
+    folded = jnp.concatenate(
+        [down_proj[one * tall : (one + 1) * tall] for one in range(pieces)], axis=1
+    )
+    return jnp.concatenate([gate_up, folded], axis=0)
+
+
+def expert_kernel(
+    arrived_ref,
+    weight_hbm,
+    out_ref,
+    weight_ref,
+    rows_ref,
+    total_ref,
+    sent_ref,
+    load_sem,
+    send_sem,
+    recv_sem,
+):
+    layers, across, block, width = arrived_ref.shape
+    shards, _, both = weight_ref.shape
+    hidden = both // 2
+    depth = HALVES * width // shards
+    fold = hidden * HDIM // both
+    tile = 2 * HDIM
     main = block // HALVES // SUB * SUB
     rest = block // HALVES - main
-    tall = sources * main
-
-    @pl.when(step == 0)
-    def _():
-        rows_ref[:tall, :width] = arrived_ref[:, :main, :].reshape(tall, width)
-        rows_ref[:tall, width:] = arrived_ref[:, main : HALVES * main, :].reshape(tall, width)
-        tail = arrived_ref[:, HALVES * main :, :].astype(jnp.float32)
-        swapped = jnp.concatenate([tail[:, rest:], tail[:, :rest]], axis=1)
-        rows_ref[tall:, :width] = tail.reshape(-1, width).astype(jnp.bfloat16)
-        rows_ref[tall:, width:] = swapped.reshape(-1, width).astype(jnp.bfloat16)
-
-    rows = rows_ref[...]
-    gate = jnp.dot(rows, gate_ref[...], preferred_element_type=jnp.float32)
-    up = jnp.dot(rows, up_ref[...], preferred_element_type=jnp.float32)
-    activated = (gate / (1.0 + jnp.exp(-gate)) * up).astype(jnp.bfloat16)
-    down = jnp.concatenate([down_ref[n] for n in range(down_ref.shape[0])], axis=1)
-    result = jnp.dot(activated, down, preferred_element_type=jnp.float32)
-
-    @pl.when(step == 0)
-    def _():
-        total_ref[...] = result
-
-    @pl.when(step > 0)
-    def _():
-        total_ref[...] = total_ref[...] + result
-
-    @pl.when(step == pl.num_programs(0) - 1)
-    def _():
-        out_ref[:, :main, :] = (
-            total_ref[:tall, :width].astype(jnp.bfloat16).reshape(sources, main, width)
+    pair = 2
+    tall = layers * main
+    low = layers * HALVES * rest
+    me = lax.axis_index("exp")
+    my_layer = me // across
+    my_place = me % across
+    loads = []
+    for part in range(4):
+        span = slice(part * shards // 4, (part + 1) * shards // 4)
+        load = pltpu.make_async_copy(weight_hbm.at[span], weight_ref.at[span], load_sem.at[part])
+        load.start()
+        loads.append(load)
+    barrier = pltpu.get_barrier_semaphore()
+    for offset in range(1, layers * across):
+        pl.semaphore_signal(
+            barrier,
+            inc=1,
+            device_id={"exp": (me + offset) % (layers * across)},
+            device_id_type=pl.DeviceIdType.MESH,
         )
-        out_ref[:, main : HALVES * main, :] = (
-            total_ref[:tall, width:].astype(jnp.bfloat16).reshape(sources, main, width)
-        )
-        left = total_ref[tall:, :width].reshape(sources, HALVES * rest, width)
-        right = total_ref[tall:, width:].reshape(sources, HALVES * rest, width)
-        out_ref[:, HALVES * main :, :] = jnp.concatenate(
-            [left[:, :rest], right[:, :rest]], axis=1
-        ).astype(jnp.bfloat16)
-
-
-def expert_local(arrived, rows_weight, cols_weight):
+    copies = []
+    for chunk in range(across // pair):
+        for one in range(pair):
+            place = (my_place + chunk * pair + one) % across
+            top = slice(one * tall, (one + 1) * tall)
+            end = slice(pair * tall + one * low, pair * tall + (one + 1) * low)
+            rows_ref[top, :width] = arrived_ref[:, place, :main, :].reshape(tall, width)
+            rows_ref[top, width:] = arrived_ref[:, place, main : HALVES * main, :].reshape(
+                tall, width
+            )
+            tail = arrived_ref[:, place, HALVES * main :, :].astype(jnp.float32)
+            swapped = jnp.concatenate([tail[:, rest:], tail[:, :rest]], axis=1)
+            rows_ref[end, :width] = tail.reshape(low, width).astype(jnp.bfloat16)
+            rows_ref[end, width:] = swapped.reshape(low, width).astype(jnp.bfloat16)
+        if chunk == 0:
+            for load in loads:
+                load.wait()
+        rows = rows_ref[...]
+        for step in range(hidden // tile):
+            at = step * tile
+            gate_weight = weight_ref[:, :depth, at : at + tile]
+            up_weight = weight_ref[:, :depth, hidden + at : hidden + at + tile]
+            gate = jnp.dot(
+                rows, gate_weight.reshape(shards * depth, tile), preferred_element_type=jnp.float32
+            )
+            up = jnp.dot(
+                rows, up_weight.reshape(shards * depth, tile), preferred_element_type=jnp.float32
+            )
+            activated = (gate / (1.0 + jnp.exp(-gate)) * up).astype(jnp.bfloat16)
+            first = at // fold
+            down = jnp.concatenate(
+                [
+                    jnp.concatenate(
+                        [
+                            weight_ref[shard, depth:, piece * HDIM : (piece + 1) * HDIM]
+                            for piece in range(first, first + tile // fold)
+                        ],
+                        axis=0,
+                    )
+                    for shard in range(shards)
+                ],
+                axis=1,
+            )
+            result = jnp.dot(activated, down, preferred_element_type=jnp.float32)
+            if step == 0:
+                total_ref[...] = result
+            else:
+                total_ref[...] = total_ref[...] + result
+        for one in range(pair):
+            turn = chunk * pair + one
+            top = slice(one * tall, (one + 1) * tall)
+            end = slice(pair * tall + one * low, pair * tall + (one + 1) * low)
+            sent_ref[turn, :, :main, :] = (
+                total_ref[top, :width].astype(jnp.bfloat16).reshape(layers, main, width)
+            )
+            sent_ref[turn, :, main : HALVES * main, :] = (
+                total_ref[top, width:].astype(jnp.bfloat16).reshape(layers, main, width)
+            )
+            left = total_ref[end, :width].reshape(layers, HALVES * rest, width)
+            right = total_ref[end, width:].reshape(layers, HALVES * rest, width)
+            sent_ref[turn, :, HALVES * main :, :] = jnp.concatenate(
+                [left[:, :rest], right[:, :rest]], axis=1
+            ).astype(jnp.bfloat16)
+        if chunk == 0:
+            pl.semaphore_wait(barrier, layers * across - 1)
+        far_first = sorted(range(layers), key=lambda hop: -min(hop, layers - hop))
+        for hop in far_first:
+            for one in range(pair):
+                turn = chunk * pair + one
+                place = (my_place + turn) % across
+                layer = (my_layer + hop) % layers
+                if turn == 0 and hop == 0:
+                    copy = pltpu.make_async_copy(
+                        sent_ref.at[turn, layer], out_ref.at[me], load_sem.at[4]
+                    )
+                else:
+                    copy = pltpu.make_async_remote_copy(
+                        src_ref=sent_ref.at[turn, layer],
+                        dst_ref=out_ref.at[me],
+                        send_sem=send_sem.at[turn, hop],
+                        recv_sem=recv_sem.at[turn, hop],
+                        device_id={"exp": layer * across + place},
+                        device_id_type=pl.DeviceIdType.MESH,
+                    )
+                copy.start()
+                copies.append(copy)
+    for copy in copies:
+        copy.wait()
+
+
+def expert_and_return(arrived, weights, across):
     sources, block, width = arrived.shape
-    main = block // HALVES // SUB * SUB
-    rest = block // HALVES - main
-    row_total = sources * (main + HALVES * rest)
-    depth, both = rows_weight.shape
-    hidden = both // 2
-    tile = 256
-    steps = hidden // tile
-    whole = pl.BlockSpec(arrived.shape, lambda j: (0, 0, 0))
+    layers = sources // across
+    both = weights.shape[2]
+    row_total = sources // across * 2 * (block // HALVES + block // HALVES % SUB)
+    outside = pl.BlockSpec(memory_space=pltpu.HBM)
     return pl.pallas_call(
         expert_kernel,
-        grid=(steps,),
         out_shape=jax.ShapeDtypeStruct(arrived.shape, jnp.bfloat16),
-        in_specs=[
-            whole,
-            pl.BlockSpec((depth, tile), lambda j: (0, j)),
-            pl.BlockSpec((depth, tile), lambda j: (0, steps + j)),
-            pl.BlockSpec((cols_weight.shape[0], tile, cols_weight.shape[2]), lambda j: (0, j, 0)),
+        in_specs=[pl.BlockSpec(memory_space=pltpu.VMEM), outside],
+        out_specs=outside,
+        scratch_shapes=[
+            pltpu.VMEM(weights.shape, jnp.bfloat16),
+            pltpu.VMEM((row_total, HALVES * width), jnp.bfloat16),
+            pltpu.VMEM((row_total, HALVES * width), jnp.float32),
+            pltpu.VMEM((across, layers, block, width), jnp.bfloat16),
+            pltpu.SemaphoreType.DMA((5,)),
+            pltpu.SemaphoreType.DMA((across, layers)),
+            pltpu.SemaphoreType.DMA((across, layers)),
         ],
-        out_specs=whole,
-        scratch_shapes=[
-            pltpu.VMEM((row_total, depth), jnp.bfloat16),
-            pltpu.VMEM((row_total, depth), jnp.float32),
-        ],
-        compiler_params=pltpu.CompilerParams(vmem_limit_bytes=48 * 1024 * 1024),
+        compiler_params=pltpu.CompilerParams(
+            collective_id=1, has_side_effects=True, vmem_limit_bytes=56 * 1024 * 1024
+        ),
         cost_estimate=pl.CostEstimate(
             flops=7 * 10**9, bytes_accessed=15 * 10**6, transcendentals=589824
         ),
-    )(arrived, rows_weight, rows_weight, cols_weight)
+    )(arrived.reshape(layers, across, block, width), weights)
 
 
 def body(
@@ -411,10 +503,7 @@
     spread, half, slot = slot_layout(experts_here, capacity)
     chosen = membership(routes, experts_here)
     codes = slot_codes(chosen, spread)
-    rows_weight, cols_weight = (
-        lax.all_gather(gate_up[0], "req", axis=0, tiled=True),
-        lax.all_gather(down_proj, "req", axis=0, tiled=True),
-    )
+    weights = lax.all_gather(pack_weights(gate_up[0], down_proj[0]), "req", axis=0)
     stream, outbox = attend_and_pack(
         new_q,
         new_kv,
@@ -430,13 +519,7 @@
     )
     outbox = outbox.reshape(experts_here, HALVES * capacity, -1)
     arrived = lax.all_to_all(outbox, "exp", split_axis=0, concat_axis=0, tiled=True)
-    returned = lax.all_to_all(
-        expert_local(arrived, rows_weight, cols_weight),
-        "exp",
-        split_axis=0,
-        concat_axis=0,
-        tiled=True,
-    )
+    returned = expert_and_return(arrived, weights, ACROSS)
     returned = returned.reshape(-1, returned.shape[-1])
     combined = combine_rows(returned, chosen, route_weight, codes, spread, half, slot)
     return (stream + combined).astype(jnp.bfloat16)

time: 204 us -> 196 us (0.961)
  the two profiles are of different devices: /device:TPU:8 before, /device:TPU:10 now
where the time goes in v4:
time: 196 us; the launch traced here: 194 us
  Pallas kernels  88.8 us (45%)
  waiting for transfers between devices  57.3 us (29%)
  between operations  14.8 us (8%)
  starting transfers between devices  13.5 us (7%)
  local copies, waits for them, and re-layouts  11.9 us (6%)
  matrix products  5.07 us (3%)
  other arithmetic  2.97 us (2%)
    pallas_call x1, Pallas kernels, expert_and_return(): pl.pallas_call(expert_kernel, out_shape=jax.ShapeDtypeStruct(arrived.shap...  71 us
    all_to_all x1, waiting for transfers between devices, body(): lax.all_to_all(outbox, 'exp', split_axis=0, concat_axis=0, tiled=True)  57.3 us
    pallas_call x1, Pallas kernels, attend_and_pack(): pl.pallas_call(attend_kernel, out_shape=(jax.ShapeDtypeStruct((tok_count,...  17.7 us
    all_to_all x1, starting transfers between devices, body(): lax.all_to_all(outbox, 'exp', split_axis=0, concat_axis=0, tiled=True)  13.5 us
    unnamed x23, local copies, waits for them, and re-layouts  10.6 us
  transfers between devices with their start and end apart: 2, of which 1 were waited for; matrix products, arithmetic and copies ran while one was open for 1% of the time, Pallas kernels for 9%

profile of v4, /device:TPU:10, one launch (start us, length us, event | category | flops | bytes accessed | tf_op | source)
XLA Modules:
  0.0 194.4 jit_solution(6136082684011625436)
XLA Ops:
  6.5 0.8 constant_dynamic-update-slice_fusion.11
  7.3 0.7 constant_dynamic-update-slice_fusion.10
  8.0 0.7 constant_dynamic-update-slice_fusion.9
  8.7 0.7 constant_dynamic-update-slice_fusion.8
  9.5 0.7 constant_dynamic-update-slice_fusion.7
  10.2 0.7 constant_dynamic-update-slice_fusion.6
  10.9 0.7 constant_dynamic-update-slice_fusion.5
  11.7 0.7 constant_dynamic-update-slice_fusion.4
  12.4 0.7 constant_dynamic-update-slice_fusion.3
  13.1 0.7 constant_dynamic-update-slice_fusion.2
  13.8 0.7 constant_dynamic-update-slice_fusion.1
  14.6 0.7 constant_dynamic-update-slice_fusion
  15.3 1.9 pad_maximum_fusion
  18.5 0.6 concatenate.21.block_ref
  19.1 17.7 %shard_map.136 = (f32[128,2048]{1,0:T(8,128)}, bf16[1280,1024]{1,0:T(8,128)(2,1)}) custom-call(s32[1]{0:T(128)S(6)} %copy.32.count_ref, bf16[8,4224]{1,0:T(8,128)(2,1)} %concatenate.21.block_ref, s32[4,128]{1,0:T(4,128)} %bitcast.37, bf16[128,2048]{1,0:T(8,128)(2,1)} %query_hbm.1, bf16[128,4096]{1,0:T(8,128)(2,1)} %own_hbm.1, bf16[128,4096]{1,0:T(8,128)(2,1)} %cache_hbm.1, ...), custom_call_target="tpu_custom_call" | custom-call | flops 2000000000 | bytes 8000000 | tf_op jit(solution)/shard_map/pallas_call | solution.py:274
  36.9 13.5 %all-to-all-start = ((bf16[32,40,1024]{2,1,0:T(8,128)(2,1)}), bf16[32,40,1024]{2,1,0:T(8,128)(2,1)S(1)}, u32[]{:S(2)}, u32[]{:S(2)}) async-start(bf16[32,40,1024]{2,1,0:T(8,128)(2,1)} %bitcast.35), calls=%async_computation | async-start | bytes 5242880 | tf_op jit(solution)/shard_map/all_to_all | solution.py:521
  50.5 0.4 fusion
  51.0 1.3 and_select_fusion.1
  52.3 57.3 %all-to-all-done = bf16[32,40,1024]{2,1,0:T(8,128)(2,1)S(1)} async-done(((bf16[32,40,1024]{2,1,0:T(8,128)(2,1)}), bf16[32,40,1024]{2,1,0:T(8,128)(2,1)S(1)}, u32[]{:S(2)}, u32[]{:S(2)}) %all-to-all-start) | async-done | bytes 2621472 | tf_op jit(solution)/shard_map/all_to_all | solution.py:521
  109.6 1.5 copy-done
  111.1 71.0 %shard_map.137 = bf16[32,40,1024]{2,1,0:T(8,128)(2,1)} custom-call(bf16[8,4,40,1024]{3,2,1,0:T(8,128)(2,1)} %bitcast.34, bf16[16,192,1536]{2,1,0:T(8,128)(2,1)} %bitcast.38), custom_call_target="tpu_custom_call" | custom-call | flops 7000000000 | bytes 15000000 | tf_op jit(solution)/shard_map/pallas_call | solution.py:463
  182.2 3.3 %fusion.1 = f32[512,1024]{1,0:T(8,128)S(1)} fusion(bf16[1280,1024]{1,0:T(8,128)(2,1)} %bitcast.40, bf16[256,1280]{1,0:T(8,128)(2,1)S(1)} %copy-done.5, bf16[256,1280]{1,0:T(8,128)(2,1)S(1)} %get-tuple-element.13), kind=kOutput, calls=%fused_computation.3 | convolution fusion | flops 1344798720 | bytes 6029312 | tf_op jit(solution)/shard_map/dot_general | solution.py:74
  185.6 1.1 copy-done.1
  186.7 0.9 fusion.6
  (19 shorter events, 0.3 us)
Async XLA Ops:
  6.5 11.9 %copy-start.2 = (bf16[8,4096]{1,0:T(8,128)(2,1)S(1)}, bf16[8,4096]{1,0:T(8,128)(2,1)}, u32[]{:S(2)}) copy-start(bf16[8,4096]{1,0:T(8,128)(2,1)} %param.18) | copy-start | bytes 196612
  6.5 103.1 %all-gather.3.cloned.1.call-start = ((), (), s32[]{:S(2)}) async-start(), calls=%async_computation.1 | async-start | bytes 10027008 | tf_op jit(solution)/shard_map/all_gather | solution.py:506
  36.9 13.6 %copy-start.3 = (s32[128,4]{0,1:T(4,128)S(1)}, s32[128,4]{0,1:T(4,128)}, u32[]{:S(2)}) copy-start(s32[128,4]{0,1:T(4,128)} %param.22) | copy-start | bytes 6148
  36.9 13.6 %copy-start.4 = (f32[128,4]{0,1:T(4,128)S(1)}, f32[128,4]{0,1:T(4,128)}, u32[]{:S(2)}) copy-start(f32[128,4]{0,1:T(4,128)} %param.23) | copy-start | bytes 6148
  36.9 72.7 %all-to-all-start = ((bf16[32,40,1024]{2,1,0:T(8,128)(2,1)}), bf16[32,40,1024]{2,1,0:T(8,128)(2,1)S(1)}, u32[]{:S(2)}, u32[]{:S(2)}) async-start(bf16[32,40,1024]{2,1,0:T(8,128)(2,1)} %bitcast.35), calls=%async_computation | async-start | bytes 5242880 | tf_op jit(solution)/shard_map/all_to_all | solution.py:521
  109.6 1.5 copy-start
  111.1 71.1 %copy-start.5 = (bf16[256,1280]{1,0:T(8,128)(2,1)S(1)}, bf16[256,1280]{1,0:T(8,128)(2,1)}, u32[]{:S(2)}) copy-start(bf16[256,1280]{1,0:T(8,128)(2,1)} %get-tuple-element.14) | copy-start | bytes 1966084
  185.5 1.2 copy-start.1
Sparse Core Ops, SparseCore 0:
  17.3 66.2 all-gather.2

commit v5 on v4

--- a/solution.py
+++ b/solution.py
@@ -314,14 +314,26 @@
     )
 
 
+def pack_weights_kernel(gate_up_ref, down_ref, out_ref):
+    depth, both = gate_up_ref.shape
+    pieces = both // HDIM
+    tall = down_ref.shape[0] // pieces
+    out_ref[:depth, :] = gate_up_ref[...]
+    for one in range(pieces):
+        out_ref[depth:, one * HDIM : (one + 1) * HDIM] = down_ref[one * tall : (one + 1) * tall, :]
+
+
 def pack_weights(gate_up, down_proj):
-    hidden = down_proj.shape[0]
-    pieces = gate_up.shape[1] // HDIM
-    tall = hidden // pieces
-    folded = jnp.concatenate(
-        [down_proj[one * tall : (one + 1) * tall] for one in range(pieces)], axis=1
-    )
-    return jnp.concatenate([gate_up, folded], axis=0)
+    depth, both = gate_up.shape
+    tall = down_proj.shape[0] * HDIM // both
+    vmem = pl.BlockSpec(memory_space=pltpu.VMEM)
+    return pl.pallas_call(
+        pack_weights_kernel,
+        out_shape=jax.ShapeDtypeStruct((depth + tall, both), gate_up.dtype),
+        in_specs=[vmem, vmem],
+        out_specs=vmem,
+        compiler_params=pltpu.CompilerParams(vmem_limit_bytes=63 * 1024 * 1024),
+    )(gate_up, down_proj)
 
 
 def expert_kernel(

time: 196 us -> 187 us (0.954)
  the two profiles are of different devices: /device:TPU:10 before, /device:TPU:34 now
where the time goes in v5:
time: 187 us
  Pallas kernels  90.7 us (49%)
  waiting for transfers between devices  57.3 us (31%)
  between operations  14.8 us (8%)
  starting transfers between devices  13.5 us (7%)
  matrix products  5.09 us (3%)
  local copies, waits for them, and re-layouts  4.03 us (2%)
    pallas_call x1, Pallas kernels, expert_and_return(): pl.pallas_call(expert_kernel, out_shape=jax.ShapeDtypeStruct(arrived.shap...  71 us
    all_to_all x1, waiting for transfers between devices, body(): lax.all_to_all(outbox, 'exp', split_axis=0, concat_axis=0, tiled=True)  57.3 us
    pallas_call x1, Pallas kernels, attend_and_pack(): pl.pallas_call(attend_kernel, out_shape=(jax.ShapeDtypeStruct((tok_count,...  17.7 us
    all_to_all x1, starting transfers between devices, body(): lax.all_to_all(outbox, 'exp', split_axis=0, concat_axis=0, tiled=True)  13.5 us
  transfers between devices with their start and end apart: 2, of which 1 were waited for; matrix products, arithmetic and copies ran while one was open for 2% of the time, Pallas kernels for 10%

profile of v5, /device:TPU:34, one launch (start us, length us, event | category | flops | bytes accessed | tf_op | source)
XLA Modules:
  0.0 186.5 jit_solution(14062949827298201218)
XLA Ops:
  6.5 0.0 all-gather.3.cloned.1.call-start
  6.5 1.9 %shard_map.137 = bf16[192,1536]{1,0:T(8,128)(2,1)} custom-call(bf16[128,1536]{1,0:T(8,128)(2,1)} %bitcast.13, bf16[768,128]{1,0:T(8,128)(2,1)} %bitcast.14), custom_call_target="tpu_custom_call" | custom-call | tf_op jit(solution)/shard_map/pallas_call | solution.py:330
  8.5 0.0 all-gather.3.cloned.1.call-update
  9.8 1.5 concatenate.15.block_ref
  11.3 17.7 %shard_map.136 = (f32[128,2048]{1,0:T(8,128)}, bf16[1280,1024]{1,0:T(8,128)(2,1)}) custom-call(s32[1]{0:T(128)S(6)} %copy.21.count_ref, bf16[8,4224]{1,0:T(8,128)(2,1)} %concatenate.15.block_ref, s32[4,128]{1,0:T(4,128)} %bitcast.15, bf16[128,2048]{1,0:T(8,128)(2,1)} %query_hbm.1, bf16[128,4096]{1,0:T(8,128)(2,1)} %own_hbm.1, bf16[128,4096]{1,0:T(8,128)(2,1)} %cache_hbm.1, ...), custom_call_target="tpu_custom_call" | custom-call | flops 2000000000 | bytes 8000000 | tf_op jit(solution)/shard_map/pallas_call | solution.py:274
  29.0 0.0 copy-start.2
  29.0 0.0 copy-start.3
  29.0 13.5 %all-to-all-start = ((bf16[32,40,1024]{2,1,0:T(8,128)(2,1)}), bf16[32,40,1024]{2,1,0:T(8,128)(2,1)S(1)}, u32[]{:S(2)}, u32[]{:S(2)}) async-start(bf16[32,40,1024]{2,1,0:T(8,128)(2,1)} %bitcast.12), calls=%async_computation | async-start | bytes 5242880 | tf_op jit(solution)/shard_map/all_to_all | solution.py:533
  42.6 0.0 copy-done.2
  42.6 0.0 copy-done.3
  42.7 0.4 fusion
  43.1 1.4 and_select_fusion.1
  44.5 57.3 %all-to-all-done = bf16[32,40,1024]{2,1,0:T(8,128)(2,1)S(1)} async-done(((bf16[32,40,1024]{2,1,0:T(8,128)(2,1)}), bf16[32,40,1024]{2,1,0:T(8,128)(2,1)S(1)}, u32[]{:S(2)}, u32[]{:S(2)}) %all-to-all-start) | async-done | bytes 2621472 | tf_op jit(solution)/shard_map/all_to_all | solution.py:533
  101.8 0.0 copy-start
  101.8 0.0 all-gather.3.cloned.1.call-done
  101.8 1.5 copy-done
  103.2 0.0 copy-start.4
  103.2 71.0 %shard_map.138 = bf16[32,40,1024]{2,1,0:T(8,128)(2,1)} custom-call(bf16[8,4,40,1024]{3,2,1,0:T(8,128)(2,1)} %bitcast.11, bf16[16,192,1536]{2,1,0:T(8,128)(2,1)} %bitcast.16), custom_call_target="tpu_custom_call" | custom-call | flops 7000000000 | bytes 15000000 | tf_op jit(solution)/shard_map/pallas_call | solution.py:475
  174.3 0.0 copy-done.4
  174.3 3.3 %fusion.1 = f32[512,1024]{1,0:T(8,128)S(1)} fusion(bf16[1280,1024]{1,0:T(8,128)(2,1)} %bitcast.18, bf16[256,1280]{1,0:T(8,128)(2,1)S(1)} %copy-done.4, bf16[256,1280]{1,0:T(8,128)(2,1)S(1)} %get-tuple-element.13), kind=kOutput, calls=%fused_computation.3 | convolution fusion | flops 1344798720 | bytes 6029312 | tf_op jit(solution)/shard_map/dot_general | solution.py:74
  177.6 0.0 copy-start.1
  177.6 0.1 slice_add_fusion.1
  177.7 1.1 copy-done.1
  178.8 0.9 fusion.6
  (5 shorter events, 0.1 us)
Async XLA Ops:
  6.5 95.2 %all-gather.3.cloned.1.call-start = ((), (), s32[]{:S(2)}) async-start(), calls=%async_computation.1 | async-start | bytes 10027008 | tf_op jit(solution)/shard_map/all_gather | solution.py:518
  29.0 13.6 %copy-start.2 = (s32[128,4]{0,1:T(4,128)S(1)}, s32[128,4]{0,1:T(4,128)}, u32[]{:S(2)}) copy-start(s32[128,4]{0,1:T(4,128)} %param.22) | copy-start | bytes 6148
  29.0 13.6 %copy-start.3 = (f32[128,4]{0,1:T(4,128)S(1)}, f32[128,4]{0,1:T(4,128)}, u32[]{:S(2)}) copy-start(f32[128,4]{0,1:T(4,128)} %param.23) | copy-start | bytes 6148
  29.0 72.7 %all-to-all-start = ((bf16[32,40,1024]{2,1,0:T(8,128)(2,1)}), bf16[32,40,1024]{2,1,0:T(8,128)(2,1)S(1)}, u32[]{:S(2)}, u32[]{:S(2)}) async-start(bf16[32,40,1024]{2,1,0:T(8,128)(2,1)} %bitcast.12), calls=%async_computation | async-start | bytes 5242880 | tf_op jit(solution)/shard_map/all_to_all | solution.py:533
  101.8 1.5 copy-start
  103.2 71.0 %copy-start.4 = (bf16[256,1280]{1,0:T(8,128)(2,1)S(1)}, bf16[256,1280]{1,0:T(8,128)(2,1)}, u32[]{:S(2)}) copy-start(bf16[256,1280]{1,0:T(8,128)(2,1)} %get-tuple-element.14) | copy-start | bytes 1966084
  177.6 1.2 copy-start.1
Sparse Core Ops, SparseCore 0:
  9.5 65.1 all-gather.2
